TPU v7x, 32 devices: a whole 2x2x4 slice. The times are simulated.
32 devices in a mesh: dp: 4 (over y, x), concept: 8 (over z, core).
Axes of the slice: x: 2, y: 2, z: 4, core: 2. Of those that a mesh axis runs over, the one named last changes fastest.
Arguments:
- embeddings: bfloat16 [32768, 1024], P(('dp', 'concept')), may hold values from -720 to 720
- row_weight: bfloat16 [32768], P(('dp', 'concept')), may hold values from 0.25 to 4
- group_label: int32 [32768, 1], P(('dp', 'concept')), may hold values from 0 to 7; in each aligned block of 1024 rows (0 to 1023, 1024 to 2047, ...) at most 256 rows name the same one
- concept_label: int32 [32768], P(('dp', 'concept')), may hold values from 0 to 1023
- level1_weight: bfloat16 [1024, 8], replicated, may hold values from -0.1875 to 0.1875
- level2_weight: bfloat16 [8, 1024, 1024], P('concept'), may hold values from -0.1875 to 0.1875
Outputs:
- row_loss: float32 [32768], P(('dp', 'concept'))
- embed_grad: bfloat16 [32768, 1024], P(('dp', 'concept'))
- level1_grad: float32 [1024, 8], replicated
- level2_grad: bfloat16 [8, 1024, 1024], P('concept', 'dp')
Inputs may be any that keep to these rules, and one draw needn't show every extreme that they name: `group_label`: among the rows of one device, no group is named more than 256 times, a bound that some block reaches.
All inputs are finite; a program needn't handle non-finite values.
Results may differ from a plain program's by a relative error of at most 0.0051.
Values may be sent and summed in bfloat16 or wider, within the bound.
No kernel may reach another device: no remote copies, remote signals or barrier semaphores. Data moves between devices by JAX's collectives and lax.ppermute only.
A program may use at most 128 MiB of HBM per device.

v0:
```python
import jax
import jax.numpy as jnp
from jax import lax
from jax.sharding import PartitionSpec as P


def first_level(embeddings, weights, groups, level1_weight):
    groups_n = level1_weight.shape[1]
    z1 = jnp.dot(embeddings, level1_weight, preferred_element_type=jnp.float32)
    top1 = jnp.max(z1, axis=1, keepdims=True)
    exps1 = jnp.exp(z1 - top1)
    total1 = jnp.sum(exps1, axis=1, keepdims=True)
    probs1 = exps1 / total1
    onehot1 = (groups[:, None] == jnp.arange(groups_n, dtype=jnp.int32)[None, :]).astype(
        jnp.float32
    )
    loss1 = top1[:, 0] + jnp.log(total1[:, 0]) - jnp.sum(z1 * onehot1, axis=1)
    dz1 = (weights[:, None] * (probs1 - onehot1)).astype(jnp.bfloat16)
    partial_grad = lax.dot_general(
        embeddings, dz1, (((0,), (0,)), ((), ())), preferred_element_type=jnp.float32
    )
    dx1 = jnp.dot(dz1, level1_weight.T, preferred_element_type=jnp.float32)
    level1_grad = lax.psum(partial_grad, ("dp", "concept"))
    return (loss1, dx1, level1_grad)


def on_device(embeddings, row_weight, group_label, concept_label, level1_weight, level2_weight):
    rows_n, width = embeddings.shape
    groups_n = level1_weight.shape[1]
    concepts = level2_weight.shape[2]
    capacity = 2 * rows_n // groups_n
    groups = group_label[:, 0]
    weights = row_weight.astype(jnp.float32)
    member = (groups[:, None] == jnp.arange(groups_n, dtype=jnp.int32)[None, :]).astype(
        jnp.bfloat16
    )
    positions = jnp.arange(rows_n, dtype=jnp.int32)
    earlier = (positions[None, :] < positions[:, None]).astype(jnp.bfloat16)
    before = jnp.dot(earlier, member, preferred_element_type=jnp.float32)
    rank = jnp.sum(before * member.astype(jnp.float32), axis=1).astype(jnp.int32)
    slot = groups * capacity + rank
    source = jnp.full((groups_n * capacity,), rows_n, jnp.int32).at[slot].set(positions)
    filled = source < rows_n
    safe = jnp.minimum(source, rows_n - 1)
    send_rows = jnp.where(filled[:, None], embeddings[safe], jnp.zeros((), jnp.bfloat16)).reshape(
        groups_n, capacity, width
    )
    send_weight = jnp.where(filled, row_weight[safe], jnp.zeros((), jnp.bfloat16)).reshape(
        groups_n, capacity
    )
    send_label = jnp.where(filled, concept_label[safe], 0).reshape(groups_n, capacity)
    loss1, dx1, level1_grad = first_level(embeddings, weights, groups, level1_weight)
    recv_rows, recv_weight, recv_label = (
        lax.all_to_all(send_rows, "concept", split_axis=0, concat_axis=1, tiled=True),
        lax.all_to_all(send_weight, "concept", split_axis=0, concat_axis=1, tiled=True),
        lax.all_to_all(send_label, "concept", split_axis=0, concat_axis=1, tiled=True),
    )
    z2 = jnp.einsum("grd,gdc->grc", recv_rows, level2_weight, preferred_element_type=jnp.float32)
    top2 = jnp.max(z2, axis=2, keepdims=True)
    exps2 = jnp.exp(z2 - top2)
    total2 = jnp.sum(exps2, axis=2, keepdims=True)
    probs2 = exps2 / total2
    onehot2 = (
        recv_label[:, :, None] == jnp.arange(concepts, dtype=jnp.int32)[None, None, :]
    ).astype(jnp.float32)
    loss2 = (top2[:, :, 0] + jnp.log(total2[:, :, 0]) - jnp.sum(z2 * onehot2, axis=2)).astype(
        jnp.bfloat16
    )
    dz2 = (recv_weight.astype(jnp.float32)[:, :, None] * (probs2 - onehot2)).astype(jnp.bfloat16)
    dx2 = jnp.einsum("grc,gdc->grd", dz2, level2_weight, preferred_element_type=jnp.float32).astype(
        jnp.bfloat16
    )
    back_grad, back_loss = (
        lax.all_to_all(dx2, "concept", split_axis=1, concat_axis=0, tiled=True),
        lax.all_to_all(loss2, "concept", split_axis=1, concat_axis=0, tiled=True),
    )
    summed = lax.psum_scatter(
        jnp.einsum("grd,grc->dgc", recv_rows, dz2, preferred_element_type=jnp.float32),
        "dp",
        scatter_dimension=0,
        tiled=True,
    )
    level2_grad = jnp.transpose(summed, (1, 0, 2)).astype(jnp.bfloat16)
    dx2_rows = back_grad.reshape(groups_n * capacity, width)[slot]
    loss2_rows = back_loss.reshape(groups_n * capacity)[slot]
    embed_grad = (dx1 + dx2_rows.astype(jnp.float32)).astype(jnp.bfloat16)
    row_loss = loss1 + loss2_rows.astype(jnp.float32)
    return (row_loss, embed_grad, level1_grad, level2_grad)


def solution(mesh):
    return jax.shard_map(
        on_device,
        mesh=mesh,
        in_specs=(
            P(("dp", "concept"), None),
            P(("dp", "concept")),
            P(("dp", "concept"), None),
            P(("dp", "concept")),
            P(),
            P("concept", None, None),
        ),
        out_specs=(P(("dp", "concept")), P(("dp", "concept"), None), P(), P("concept", "dp", None)),
        check_vma=False,
    )
```

profile of v0, /device:TPU:0, one launch (start us, length us, event | category | flops | bytes accessed | tf_op | source)
XLA Modules:
  0.0 421.7 jit_solution(6824636984605057728)
XLA Ops:
  7.2 0.0 copy-start
  7.2 1.3 fusion.6
  8.5 0.7 compare_select_fusion
  9.2 4.3 %scatter_custom_fusion = s32[2048]{0:T(1024)S(1)} fusion(s32[1024]{0:T(1024)S(1)} %bitcast.59, s32[1024]{0:T(1024)S(1)} %iota.19, s32[]{:T(128)} %constant.2.clone.1), kind=kCustom, calls=%fused_computation.39 | custom fusion | bytes 8196 | tf_op jit(solution)/shard_map/scatter | solution.py:42
  13.6 11.5 %gather_fusion.3 = bf16[2048]{0:T(1024)(128)(2,1)S(1)} fusion(bf16[1024]{0:T(1024)(128)(2,1)} %param.7, s32[2048]{0:T(1024)S(1)} %fusion.10), kind=kCustom, calls=%fused_computation.3 | custom fusion | bytes 16384 | tf_op jit(solution)/shard_map/gather | solution.py:48
  25.1 0.5 broadcast.72
  25.6 0.7 reduce.9
  26.3 0.6 reshape.239
  26.9 6.4 %all-to-all-start.3 = ((bf16[8,2,128]{2,1,0:T(2,128)(2,1)}), bf16[8,2,128]{2,1,0:T(2,128)(2,1)S(1)}, u32[]{:S(2)}, u32[]{:S(2)}) async-start(bf16[8,2,128]{2,1,0:T(2,128)(2,1)} %reshape.239), calls=%async_computation.3 | async-start | bytes 8192 | tf_op jit(solution)/shard_map/all_to_all | solution.py:55
  33.2 12.8 %gather_fusion = bf16[2048,1024]{1,0:T(8,128)(2,1)} fusion(bf16[1024,1024]{1,0:T(8,128)(2,1)} %param.6, s32[2048]{0:T(1024)S(1)} %fusion.10), kind=kCustom, calls=%fused_computation | custom fusion | bytes 8396800 | tf_op jit(solution)/shard_map/gather | solution.py:45
  46.1 3.8 broadcast_select_fusion
  49.9 0.0 all-to-all-done.3
  49.9 5.2 %all-to-all-start = ((bf16[8,256,1024]{2,1,0:T(8,128)(2,1)}), bf16[8,256,1024]{2,1,0:T(8,128)(2,1)}, u32[]{:S(2)}, u32[]{:S(2)}) async-start(bf16[8,256,1024]{2,1,0:T(8,128)(2,1)} %broadcast_select_fusion), calls=%async_computation | async-start | bytes 8388608 | tf_op jit(solution)/shard_map/all_to_all | solution.py:54
  55.1 0.0 copy-done.2
  55.1 8.6 %gather_fusion.1 = s32[2048]{0:T(1024)S(1)} fusion(s32[1024]{0:T(1024)S(1)} %copy-done.2, s32[2048]{0:T(1024)S(1)} %fusion.10), kind=kCustom, calls=%fused_computation.1 | custom fusion | bytes 24576 | tf_op jit(solution)/shard_map/gather | solution.py:51
  63.7 0.6 broadcast_select_fusion.1
  64.3 84.9 %all-to-all-done = bf16[8,256,1024]{2,1,0:T(8,128)(2,1)} async-done(((bf16[8,256,1024]{2,1,0:T(8,128)(2,1)}), bf16[8,256,1024]{2,1,0:T(8,128)(2,1)}, u32[]{:S(2)}, u32[]{:S(2)}) %all-to-all-start) | async-done | bytes 4194336 | tf_op jit(solution)/shard_map/all_to_all | solution.py:54
  149.2 3.3 all-to-all-start.1
  152.5 0.0 reduce-scatter.2.cloned.1.call-start
  152.6 9.0 %fusion.13 = (f32[2048]{0:T(1024)S(1)}, f32[2048,1024]{0,1:T(8,128)}) fusion(bf16[2048,1024]{1,0:T(8,128)(2,1)} %bitcast.4, bf16[1,1024,1024]{2,1,0:T(8,128)(2,1)S(1)} %copy-done), kind=kOutput, calls=%fused_computation.43 | convolution fusion | flops 4297062400 | bytes 14688256 | tf_op jit(solution)/shard_map/grd,gdc->grc/dot_general | solution.py:58
  161.6 0.0 all-to-all-done.1
  161.6 4.7 %fusion = (f32[2048]{0:T(1024)S(1)}, f32[2048]{0:T(1024)S(1)}) fusion(f32[2048,1024]{0,1:T(8,128)} %get-tuple-element.27, f32[2048]{0:T(1024)S(1)} %get-tuple-element.26, s32[2048]{0:T(1024)S(1)} %bitcast.51), kind=kLoop, calls=%fused_computation.10 | loop fusion | flops 10481664 | bytes 8421376 | tf_op jit(solution)/shard_map/reduce_sum | solution.py:61
  166.3 1.1 copy-done.4
  167.4 2.6 multiply_convert_fusion
  170.1 1.9 copy-done.5
  172.0 8.2 %convolution_bitcast_fusion = f32[1024,1,1024]{0,2,1:T(8,128)} fusion(bf16[2048,1024]{0,1:T(8,128)(2,1)S(1)} %multiply_convert_fusion, bf16[2048,1024]{1,0:T(8,128)(2,1)} %bitcast.4), kind=kOutput, calls=%fused_computation.17 | convolution fusion | flops 4294967296 | bytes 12582912 | tf_op jit(solution)/shard_map/grd,grc->dgc/dot_general | solution.py:78
  180.1 0.0 reduce-scatter.2.cloned.1.call-update
  180.1 0.7 reduce.8
  180.8 0.6 reshape.237
  181.4 5.0 %all-to-all-start.2 = ((bf16[8,2,128]{2,1,0:T(2,128)(2,1)}), bf16[8,2,128]{2,1,0:T(2,128)(2,1)S(1)}, u32[]{:S(2)}, u32[]{:S(2)}) async-start(bf16[8,2,128]{2,1,0:T(2,128)(2,1)} %reshape.237), calls=%async_computation.2 | async-start | bytes 8192 | tf_op jit(solution)/shard_map/all_to_all | solution.py:75
  186.4 7.5 %convert_bitcast_fusion = bf16[1,2048,1024]{2,1,0:T(8,128)(2,1)S(1)} fusion(bf16[2048,1024]{0,1:T(8,128)(2,1)} %copy-done.5, bf16[1,1024,1024]{2,1,0:T(8,128)(2,1)S(1)} %copy-done), kind=kOutput, calls=%fused_computation.13 | convolution fusion | flops 4297064448 | bytes 10485760 | tf_op jit(solution)/shard_map/grc,gdc->grd/dot_general | solution.py:70
  193.9 28.7 %copy.24 = bf16[1,2048,1024]{2,0,1:T(2,128)(2,1)} copy(bf16[1,2048,1024]{2,1,0:T(8,128)(2,1)S(1)} %convert_bitcast_fusion) | data formatting | bytes 8388608 | tf_op jit(solution)/shard_map/convert_element_type | solution.py:70
  222.6 26.0 %reduce.10 = bf16[2048,1024]{1,0:T(8,128)(2,1)} reduce(bf16[2048,1,1024]{2,1,0:T(2,128)(2,1)} %bitcast.48, bf16[]{:T(256)} %broadcast.72), dimensions={1}, to_apply=%bitcast.44.reduce_sub_computation | reduce | bytes 8388610
  248.6 7.8 %reshape.241 = bf16[8,2,131072]{2,1,0:T(2,128)(2,1)} reshape(bf16[2048,1024]{1,0:T(8,128)(2,1)} %reduce.10) | data formatting | bytes 8388608
  256.4 0.0 all-to-all-done.2
  256.4 5.3 %all-to-all-start.4 = ((bf16[8,2,131072]{2,1,0:T(2,128)(2,1)}), bf16[8,2,131072]{2,1,0:T(2,128)(2,1)}, u32[]{:S(2)}, u32[]{:S(2)}) async-start(bf16[8,2,131072]{2,1,0:T(2,128)(2,1)} %reshape.241), calls=%async_computation.4 | async-start | bytes 8388608 | tf_op jit(solution)/shard_map/all_to_all | solution.py:74
  261.8 2.3 fusion.14
  264.1 2.0 convolution_bitcast_fusion.1
  266.1 110.7 %psum.7 = f32[1024,8]{0,1:T(8,128)} all-reduce(f32[1024,8]{0,1:T(8,128)S(1)} %convolution_bitcast_fusion.1), channel_id=1, replica_groups=mesh['dp'=4,'concept'=8] {'dp','concept'}, use_global_device_ids=true, to_apply=%region_8.9 | all-reduce | flops 8192 | bytes 65536 | tf_op jit(solution)/shard_map/psum | solution.py:23
  376.8 6.8 %gather_fusion.2 = bf16[1024]{0:T(1024)(128)(2,1)S(1)} fusion(bf16[2048]{0:T(1024)(128)(2,1)S(1)} %bitcast.46, s32[1024]{0:T(1024)S(1)} %broadcast_clamp_fusion), kind=kCustom, calls=%fused_computation.2 | custom fusion | bytes 8192 | tf_op jit(solution)/shard_map/gather | solution.py:85
  383.6 0.6 convert_add_fusion
  384.2 0.0 all-to-all-done.4
  384.2 8.8 %reshape.242 = bf16[2048,1,1024]{2,1,0:T(2,128)(2,1)} reshape(bf16[8,2,131072]{2,1,0:T(2,128)(2,1)} %all-to-all-done.4) | data formatting | bytes 8388608
  393.0 7.0 %copy.23 = bf16[1,2048,1024]{2,1,0:T(8,128)(2,1)} copy(bf16[1,2048,1024]{2,0,1:T(2,128)(2,1)} %bitcast.49) | data formatting | bytes 8388608
  400.0 8.9 %gather_fusion.4 = bf16[1024,1024]{1,0:T(8,128)(2,1)} fusion(bf16[2048,1024]{1,0:T(8,128)(2,1)} %bitcast.47, s32[1024]{0:T(1024)S(1)} %broadcast_clamp_fusion), kind=kCustom, calls=%fused_computation.4 | custom fusion | bytes 4198400 | tf_op jit(solution)/shard_map/gather | solution.py:84
  408.9 3.7 add_convert_fusion
  412.6 1.3 convert_bitcast_fusion.1
  413.8 1.0 copy.18
  (29 shorter events, 0.2 us)
Async XLA Ops:
  7.2 145.4 %copy-start = (bf16[1,1024,1024]{2,1,0:T(8,128)(2,1)S(1)}, bf16[1,1024,1024]{2,1,0:T(8,128)(2,1)}, u32[]{:S(2)}) copy-start(bf16[1,1024,1024]{2,1,0:T(8,128)(2,1)} %param.11) | copy-start | bytes 6291460
  26.9 23.0 %all-to-all-start.3 = ((bf16[8,2,128]{2,1,0:T(2,128)(2,1)}), bf16[8,2,128]{2,1,0:T(2,128)(2,1)S(1)}, u32[]{:S(2)}, u32[]{:S(2)}) async-start(bf16[8,2,128]{2,1,0:T(2,128)(2,1)} %reshape.239), calls=%async_computation.3 | async-start | bytes 8192 | tf_op jit(solution)/shard_map/all_to_all | solution.py:55
  49.9 5.2 %copy-start.2 = (s32[1024]{0:T(1024)S(1)}, s32[1024]{0:T(1024)}, u32[]{:S(2)}) copy-start(s32[1024]{0:T(1024)} %param.9) | copy-start | bytes 12292
  49.9 99.3 %all-to-all-start = ((bf16[8,256,1024]{2,1,0:T(8,128)(2,1)}), bf16[8,256,1024]{2,1,0:T(8,128)(2,1)}, u32[]{:S(2)}, u32[]{:S(2)}) async-start(bf16[8,256,1024]{2,1,0:T(8,128)(2,1)} %broadcast_select_fusion), calls=%async_computation | async-start | bytes 8388608 | tf_op jit(solution)/shard_map/all_to_all | solution.py:54
  149.2 12.4 %all-to-all-start.1 = ((s32[8,1,256]{2,1,0:T(1,128)}), s32[8,1,256]{2,1,0:T(1,128)S(1)}, u32[]{:S(2)}, u32[]{:S(2)}) async-start(s32[8,1,256]{2,1,0:T(1,128)} %bitcast.6), calls=%async_computation.1 | async-start | bytes 16384 | tf_op jit(solution)/shard_map/all_to_all | solution.py:56
  152.5 260.0 %reduce-scatter.2.cloned.1.call-start = ((), (), s32[]{:S(2)}) async-start(), calls=%async_computation.6 | async-start | bytes 5242880 | tf_op jit(solution)/shard_map/reduce_scatter | solution.py:77
  161.6 5.8 %copy-start.4 = (f32[2048,1024]{0,1:T(8,128)S(1)}, f32[2048,1024]{0,1:T(8,128)}, u32[]{:S(2)}) copy-start(f32[2048,1024]{0,1:T(8,128)} %get-tuple-element.27) | copy-start | bytes 25165828
  170.0 1.9 copy-start.5
  181.4 75.0 %all-to-all-start.2 = ((bf16[8,2,128]{2,1,0:T(2,128)(2,1)}), bf16[8,2,128]{2,1,0:T(2,128)(2,1)S(1)}, u32[]{:S(2)}, u32[]{:S(2)}) async-start(bf16[8,2,128]{2,1,0:T(2,128)(2,1)} %reshape.237), calls=%async_computation.2 | async-start | bytes 8192 | tf_op jit(solution)/shard_map/all_to_all | solution.py:75
  256.4 5.3 %copy-start.3 = (bf16[1024]{0:T(1024)(128)(2,1)S(1)}, bf16[1024]{0:T(1024)(128)(2,1)}, u32[]{:S(2)}) copy-start(bf16[1024]{0:T(1024)(128)(2,1)} %param.7) | copy-start | bytes 6148
  256.4 5.4 %copy-start.6 = (bf16[1024,8]{0,1:T(8,128)(2,1)S(1)}, bf16[1024,8]{0,1:T(8,128)(2,1)}, u32[]{:S(2)}) copy-start(bf16[1024,8]{0,1:T(8,128)(2,1)} %param.10) | copy-start | bytes 49156
  256.4 7.6 %copy-start.7 = (s32[1024,1]{0,1:T(1,128)S(1)}, s32[1024,1]{0,1:T(1,128)}, u32[]{:S(2)}) copy-start(s32[1024,1]{0,1:T(1,128)} %param.8) | copy-start | bytes 12292
  256.4 127.8 %all-to-all-start.4 = ((bf16[8,2,131072]{2,1,0:T(2,128)(2,1)}), bf16[8,2,131072]{2,1,0:T(2,128)(2,1)}, u32[]{:S(2)}, u32[]{:S(2)}) async-start(bf16[8,2,131072]{2,1,0:T(2,128)(2,1)} %reshape.241), calls=%async_computation.4 | async-start | bytes 8388608 | tf_op jit(solution)/shard_map/all_to_all | solution.py:74
  400.0 14.8 %copy-start.1 = (bf16[1,1024,1024]{2,1,0:T(8,128)(2,1)S(1)}, bf16[1,1024,1024]{2,1,0:T(8,128)(2,1)}, u32[]{:S(2)}) copy-start(bf16[1,1024,1024]{2,1,0:T(8,128)(2,1)} %param.11) | copy-start | bytes 6291460
Sparse Core Ops, SparseCore 0:
  180.3 53.9 reduce-scatter.1
where the time goes:
time: 423 us; the launch traced here: 422 us
  local copies, waits for them, and re-layouts  111 us (26%)
  blocking collectives  111 us (26%)
  waiting for transfers between devices  84.9 us (20%)
  other arithmetic  41.7 us (10%)
  matrix products  33.9 us (8%)
  starting transfers between devices  25.3 us (6%)
  between operations  14.2 us (3%)
    psum x1, blocking collectives, first_level(): level1_grad = lax.psum(partial_grad, ('dp', 'concept'))  111 us
    all_to_all x1, waiting for transfers between devices, on_device(): lax.all_to_all(send_rows, 'concept', split_axis=0, concat_axis=1, tiled=T...  84.9 us
    unnamed x26, local copies, waits for them, and re-layouts  29.4 us
    convert_element_type x1, local copies, waits for them, and re-layouts, on_device(): jnp.einsum('grc,gdc->grd', dz2, level2_weight, preferred_element_type=jnp...  28.7 us
    unnamed x2, other arithmetic  26.6 us
    gather x1, local copies, waits for them, and re-layouts, on_device(): embeddings[safe]  12.8 us
    gather x1, local copies, waits for them, and re-layouts, on_device(): row_weight[safe]  11.5 us
    dot_general x1, matrix products, on_device(): jnp.einsum('grd,gdc->grc', recv_rows, level2_weight, preferred_element_ty...  9.01 us
  transfers between devices with their start and end apart: 6, of which 1 were waited for; matrix products, arithmetic and copies ran while one was open for 35% of the time, Pallas kernels for 0%

commit v1 on v0

--- a/solution.py
+++ b/solution.py
@@ -1,7 +1,14 @@
 import jax
 import jax.numpy as jnp
 from jax import lax
+from jax.experimental import pallas as pl
+from jax.experimental.pallas import tpu as pltpu
 from jax.sharding import PartitionSpec as P
+
+LANES = 128
+PIECES = 2
+F32, BF16 = jnp.float32, jnp.bfloat16
+AXES = ("dp", "concept")
 
 
 def first_level(embeddings, weights, groups, level1_weight):
@@ -88,9 +95,437 @@
     return (row_loss, embed_grad, level1_grad, level2_grad)
 
 
+def nn(a, b):
+    return lax.dot_general(a, b, (((1,), (0,)), ((), ())), preferred_element_type=F32)
+
+
+def nt(a, b):
+    return lax.dot_general(a, b, (((1,), (1,)), ((), ())), preferred_element_type=F32)
+
+
+def tn(a, b):
+    return lax.dot_general(a, b, (((0,), (0,)), ((), ())), preferred_element_type=F32)
+
+
+def upright(row):
+    return jnp.transpose(jnp.broadcast_to(row, (LANES, row.shape[1])))[:, 0:1]
+
+
+def near_kernel(
+    me_ref, group_ref, label_ref, weight_ref, rows_ref, theirs_ref, mine_ref, key_ref, aux_ref
+):
+    cap, _ = mine_ref.shape
+    rows_n, _ = rows_ref.shape
+    groups_n = 2 * rows_n // cap
+    groups = group_ref[...]
+    kinds = lax.broadcasted_iota(jnp.int32, (groups_n, rows_n), 0)
+    hot = jnp.where(groups == kinds, 1.0, 0.0)
+    earlier = lax.broadcasted_iota(jnp.int32, (rows_n, rows_n), 0) < lax.broadcasted_iota(
+        jnp.int32, (rows_n, rows_n), 1
+    )
+    before = nn(hot.astype(BF16), jnp.where(earlier, 1.0, 0.0).astype(BF16))
+    rank = jnp.sum(before * hot, axis=0, keepdims=True).astype(jnp.int32)
+    key_ref[...] = (groups ^ me_ref[0]) * cap + rank
+    kind = lax.broadcasted_iota(jnp.int32, (LANES, rows_n), 0)
+    label = label_ref[...]
+    weight = weight_ref[...].astype(F32)
+    high = (label >> 5).astype(F32)
+    low = (label & 31).astype(F32)
+    aux_ref[...] = jnp.where(
+        kind == 0, weight, jnp.where(kind == 1, high, jnp.where(kind == 2, low, 0.0))
+    ).astype(BF16)
+    place_rows(key_ref, aux_ref, rows_ref, mine_ref, 2)
+    place_rows(key_ref, aux_ref, rows_ref, theirs_ref, 3)
+
+
+def place_rows(key_ref, aux_ref, rows_ref, out_ref, t):
+    cap = out_ref.shape[0]
+    rows_n, width = rows_ref.shape
+    place = lax.broadcasted_iota(jnp.int32, (cap, rows_n), 0)
+    pick = jnp.where(key_ref[...] == place + t * cap, 1.0, 0.0).astype(BF16)
+    out_ref[:, :width] = nn(pick, rows_ref[...]).astype(BF16)
+    out_ref[:, width:] = nt(pick, aux_ref[...]).astype(BF16)
+
+
+def near_rows(me, groups, labels, weights, rows, cap):
+    rows_n, width = rows.shape
+    full = width + LANES
+    vmem = pl.BlockSpec(memory_space=pltpu.VMEM)
+    out = jax.ShapeDtypeStruct((cap, full), BF16)
+    return pl.pallas_call(
+        near_kernel,
+        in_specs=[pl.BlockSpec(memory_space=pltpu.SMEM)] + [vmem] * 4,
+        out_specs=[vmem] * 4,
+        out_shape=[
+            out,
+            out,
+            jax.ShapeDtypeStruct((1, rows_n), jnp.int32),
+            jax.ShapeDtypeStruct((LANES, rows_n), BF16),
+        ],
+        cost_estimate=pl.CostEstimate(
+            flops=6 * cap * rows_n * full,
+            bytes_accessed=2 * (rows_n * width + 2 * cap * full),
+            transcendentals=0,
+        ),
+        name="near_rows",
+    )(me, groups, labels, weights, rows)
+
+
+def prepare_kernel(
+    key_ref, aux_ref, group_ref, weight_ref, w1_ref, rows_ref,
+    theirs_ref, mine_ref, loss_ref, dz_ref, grad_ref,
+):
+    s = pl.program_id(0)
+    slot = jnp.where(s == 0, 0, s + 1)
+    groups_n = w1_ref.shape[0]
+    rows_n = rows_ref.shape[0]
+    place_rows(key_ref, aux_ref, rows_ref, theirs_ref, 2 * slot + 1)
+    place_rows(key_ref, aux_ref, rows_ref, mine_ref, 2 * slot)
+
+    @pl.when(s == 0)
+    def _():
+        kinds = lax.broadcasted_iota(jnp.int32, (groups_n, rows_n), 0)
+        hot = jnp.where(group_ref[...] == kinds, 1.0, 0.0)
+        weight = weight_ref[...].astype(F32)
+        z = nt(w1_ref[...], rows_ref[...])
+        top = jnp.max(z, axis=0, keepdims=True)
+        exps = jnp.exp(z - top)
+        mass = jnp.sum(exps, axis=0, keepdims=True)
+        loss_ref[...] = top + jnp.log(mass) - jnp.sum(z * hot, axis=0, keepdims=True)
+        dz = (weight * (exps / mass - hot)).astype(BF16)
+        dz_ref[...] = dz
+        grad_ref[...] = nn(dz, rows_ref[...])
+
+
+def prepare(key, aux, groups, weights, w1, rows, cap):
+    rows_n, width = rows.shape
+    groups_n = w1.shape[0]
+    full = width + LANES
+    slots = groups_n // 2 - 1
+    out = jax.ShapeDtypeStruct((slots, cap, full), BF16)
+    block = pl.BlockSpec((pl.Squeezed(), cap, full), lambda s: (s, 0, 0))
+    flat = lambda *shape: pl.BlockSpec(shape, lambda s: (0, 0))
+    line = flat(1, rows_n)
+    return pl.pallas_call(
+        prepare_kernel,
+        grid=(slots,),
+        in_specs=[
+            line, flat(LANES, rows_n), line, line, flat(groups_n, width), flat(rows_n, width),
+        ],
+        out_specs=[block, block, line, flat(groups_n, rows_n), flat(groups_n, width)],
+        out_shape=[
+            out,
+            out,
+            jax.ShapeDtypeStruct((1, rows_n), F32),
+            jax.ShapeDtypeStruct((groups_n, rows_n), BF16),
+            jax.ShapeDtypeStruct((groups_n, width), F32),
+        ],
+        cost_estimate=pl.CostEstimate(
+            flops=4 * slots * cap * rows_n * full,
+            bytes_accessed=2 * (rows_n * width + 2 * slots * cap * full),
+            transcendentals=0,
+        ),
+        name="prepare",
+    )(key, aux, groups, weights, w1, rows)
+
+
+def rows_kernel(picks, n_pieces, n_extra, cap, with_grads, meta_ref, *refs):
+    n_blocks = len(picks)
+    blocks, refs = refs[:n_blocks], refs[n_blocks:]
+    pieces, refs = refs[:n_pieces], refs[n_pieces:]
+    extra, refs = refs[:n_extra], refs[n_extra:]
+    outs, refs = refs[:n_blocks], refs[n_blocks:]
+    if with_grads:
+        grad_outs, refs = refs[:4], refs[4:]
+        x_s, w_s, dz_s, dx_s, g_s, sems = refs
+    else:
+        dz_out, refs = refs[0], refs[1:]
+        x_s, w_s, dz_s, dx_s, sems = refs
+    width, concepts = w_s.shape
+    total = n_blocks * cap
+    copies = []
+
+    def start(src, dst, n):
+        copies.append(pltpu.make_async_copy(src, dst, sems.at[n]))
+        copies[-1].start()
+
+    def drain():
+        for copy in copies:
+            copy.wait()
+        copies.clear()
+
+    for i, piece in enumerate(pieces):
+        at = pl.multiple_of(meta_ref[i], LANES)
+        start(piece, w_s.at[pl.ds(at, piece.shape[0])], i)
+    for i, (block, pick) in enumerate(zip(blocks, picks)):
+        src = block if pick is None else block.at[pick]
+        start(src, x_s.at[pl.ds(i * cap, cap)], n_pieces + i)
+    drain()
+    for i, block in enumerate(extra[:-1]):
+        start(block, x_s.at[pl.ds(total + i * cap, cap)], i)
+    if extra:
+        start(extra[-1], dz_s.at[pl.ds(total, extra[-1].shape[0])], n_extra)
+    later = list(copies)
+    copies.clear()
+    column = lax.broadcasted_iota(jnp.int32, (cap, concepts), 1)
+
+    @pl.loop(0, n_blocks)
+    def _(b):
+        here = pl.ds(pl.multiple_of(b * cap, cap), cap)
+        z = nn(x_s[here, :width], w_s[...])
+        aux = x_s[here, width:].astype(F32)
+        weight = aux[:, 0:1]
+        label = (aux[:, 1:2] * 32.0 + aux[:, 2:3]).astype(jnp.int32)
+        hot = column == label
+        top = jnp.max(z, axis=1, keepdims=True)
+        exps = jnp.exp(z - top)
+        mass = jnp.sum(exps, axis=1, keepdims=True)
+        picked = jnp.sum(jnp.where(hot, z, 0.0), axis=1, keepdims=True)
+        probs = exps * (1.0 / mass)
+        dz = (weight * (probs - jnp.where(hot, 1.0, 0.0))).astype(BF16)
+        dz_s[here, :] = dz
+        dx_s[here, :width] = nt(dz, w_s[...]).astype(BF16)
+        loss = top + jnp.log(mass) - picked
+        dx_s[here, width:] = jnp.broadcast_to(loss, (cap, LANES)).astype(BF16)
+
+    for copy in later:
+        copy.wait()
+    for i, out in enumerate(outs):
+        start(dx_s.at[pl.ds(i * cap, cap)], out, i)
+    if not with_grads:
+        start(dz_s, dz_out, n_blocks)
+    else:
+        quarter, part = g_s.shape[1], g_s.shape[2]
+        for j in range(8):
+            at = pl.multiple_of(meta_ref[n_pieces + j], LANES)
+            half = (0, 0, 1, 1, 0, 0, 1, 1)[j]
+            g_s[j] = tn(
+                x_s[:, pl.ds(at, quarter)], dz_s[:, half * part : (half + 1) * part]
+            ).astype(BF16)
+            if j % 2 == 1:
+                start(g_s.at[pl.ds(j - 1, 2)], grad_outs[j // 2], n_blocks + j // 2)
+    drain()
+
+
+def group_step(blocks, pieces, starts, quarters, concepts, cap, extra=(), with_grads=True):
+    full = blocks[0][0].shape[-1]
+    width = full - LANES
+    own_rows = cap * len(blocks)
+    total = own_rows + cap * max(len(extra) - 1, 0)
+    quarter, part = width // 4, concepts // 2
+    meta = jnp.stack(starts + [q * quarter for q in quarters]).astype(jnp.int32)
+    hbm = pl.BlockSpec(memory_space=pltpu.HBM)
+    dx = jax.ShapeDtypeStruct((cap, full), BF16)
+    if with_grads:
+        rest = [jax.ShapeDtypeStruct((2, quarter, part), BF16)] * 4
+        grad_scratch = [pltpu.VMEM((8, quarter, part), BF16)]
+    else:
+        rest = [jax.ShapeDtypeStruct((total, concepts), BF16)]
+        grad_scratch = []
+    n_sems = max(len(pieces) + len(blocks), len(blocks) + 4, len(extra) + 1)
+    picks = [i for _, i in blocks]
+    res = pl.pallas_call(
+        lambda *refs: rows_kernel(picks, len(pieces), len(extra), cap, with_grads, *refs),
+        in_specs=[pl.BlockSpec(memory_space=pltpu.SMEM)]
+        + [hbm] * (len(blocks) + len(pieces) + len(extra)),
+        out_specs=[hbm] * (len(blocks) + len(rest)),
+        out_shape=[dx] * len(blocks) + rest,
+        scratch_shapes=[
+            pltpu.VMEM((total, full), BF16),
+            pltpu.VMEM((width, concepts), BF16),
+            pltpu.VMEM((total, concepts), BF16),
+            pltpu.VMEM((own_rows, full), BF16),
+            *grad_scratch,
+            pltpu.SemaphoreType.DMA((n_sems,)),
+        ],
+        cost_estimate=pl.CostEstimate(
+            flops=(4 * own_rows + 2 * total * with_grads) * width * concepts,
+            bytes_accessed=4 * (total * full + width * concepts),
+            transcendentals=own_rows * concepts,
+        ),
+    )(meta, *[a for a, _ in blocks], *pieces, *extra)
+    return res[: len(blocks)], res[len(blocks) :]
+
+
+def combine_kernel(n_blocks, cap, key_ref, loss_ref, dz1_ref, w1_ref, *refs):
+    blocks, refs = refs[:n_blocks], refs[n_blocks:]
+    out_ref, row_loss_ref, x_s, sems = refs
+
+    @pl.when(pl.program_id(0) == 0)
+    def _():
+        copies = [
+            pltpu.make_async_copy(b, x_s.at[pl.ds(i * cap, cap)], sems.at[i])
+            for i, b in enumerate(blocks)
+        ]
+        for copy in copies:
+            copy.start()
+        for copy in copies:
+            copy.wait()
+
+    tile, width = out_ref.shape
+    slots = x_s.shape[0]
+    place = lax.broadcasted_iota(jnp.int32, (tile, slots), 1)
+    pick = jnp.where(upright(key_ref[...]) == place, 1.0, 0.0).astype(BF16)
+    got = nn(pick, x_s[...])
+    dx1 = tn(dz1_ref[...], w1_ref[...])
+    out_ref[...] = (dx1 + got[:, :width]).astype(BF16)
+    row_loss_ref[...] = loss_ref[...] + jnp.transpose(got[:, width:])[0:1, :]
+
+
+def combine(key, loss1, dz1, w1, blocks, cap):
+    rows_n = key.shape[1]
+    groups_n, width = w1.shape
+    full = width + LANES
+    tile = cap
+    slots = cap * len(blocks)
+    line = pl.BlockSpec((1, tile), lambda i: (0, i))
+    return pl.pallas_call(
+        lambda *refs: combine_kernel(len(blocks), cap, *refs),
+        grid=(rows_n // tile,),
+        in_specs=[
+            line,
+            line,
+            pl.BlockSpec((groups_n, tile), lambda i: (0, i)),
+            pl.BlockSpec((groups_n, width), lambda i: (0, 0)),
+        ]
+        + [pl.BlockSpec(memory_space=pltpu.HBM)] * len(blocks),
+        out_specs=[pl.BlockSpec((tile, width), lambda i: (i, 0)), line],
+        out_shape=[
+            jax.ShapeDtypeStruct((rows_n, width), BF16),
+            jax.ShapeDtypeStruct((1, rows_n), F32),
+        ],
+        scratch_shapes=[
+            pltpu.VMEM((slots, full), BF16),
+            pltpu.SemaphoreType.DMA((len(blocks),)),
+        ],
+        cost_estimate=pl.CostEstimate(
+            flops=2 * rows_n * slots * full,
+            bytes_accessed=2 * (slots * full + rows_n * width),
+            transcendentals=0,
+        ),
+        name="combine",
+    )(key, loss1, dz1, w1, *blocks)
+
+
+def make_local(dp_n, concept_n):
+    def pairs(dp_bit, concept_bit):
+        return [
+            (d * concept_n + c, (d ^ dp_bit) * concept_n + (c ^ concept_bit))
+            for d in range(dp_n)
+            for c in range(concept_n)
+        ]
+
+    core, near, cross, far, away, side, up = (
+        pairs(0, 1),
+        pairs(0, 2),
+        pairs(0, 3),
+        pairs(0, 4),
+        pairs(0, 6),
+        pairs(1, 0),
+        pairs(2, 0),
+    )
+
+    def send(a, to):
+        return lax.ppermute(a, AXES, to)
+
+    def local(embeddings, row_weight, group_label, concept_label, level1_weight, level2_weight):
+        return body(
+            embeddings, row_weight, group_label, concept_label, level1_weight, level2_weight
+        )
+
+    def body(embeddings, row_weight, group_label, concept_label, level1_weight, level2_weight):
+        rows_n, width = embeddings.shape
+        groups_n = level1_weight.shape[1]
+        concepts = level2_weight.shape[2]
+        cap = 2 * rows_n // groups_n
+        quarter = width // dp_n
+        piece = quarter // PIECES
+        dp, me = lax.axis_index("dp"), lax.axis_index("concept")
+
+        own = level2_weight[0]
+
+        def spread(q, h):
+            qx, qy = send(q, side), send(q, up)
+            last = send(qx, up) if h % 2 == 0 else send(qy, side)
+            return [q, qx, qy, last]
+
+        pieces2, pieces3, starts = [], [], []
+        for h in range(PIECES):
+            first = lax.dynamic_slice_in_dim(own, dp * quarter + h * piece, piece, 0)
+            far2 = send(first, far)
+            far3 = send(far2, near)
+            pieces2 += spread(far2, h)
+            pieces3 += spread(far3, h)
+            starts += [(dp ^ i) * quarter + h * piece for i in range(4)]
+        order = [dp ^ 1, dp ^ 3, dp ^ 2, dp ^ 3, dp, dp ^ 2, dp, dp ^ 1]
+
+        w1 = level1_weight.T
+        groups, weights = group_label.T, row_weight[None, :]
+        theirs1, mine1, key, aux = near_rows(
+            me[None].astype(jnp.int32),
+            groups,
+            concept_label[None, :],
+            weights,
+            embeddings,
+            cap,
+        )
+        rows_in = [send(mine1, near), send(theirs1, cross)]
+        theirs, mine, loss1, dz1, grad1 = prepare(key, aux, groups, weights, w1, embeddings, cap)
+        got = send(theirs, core)
+        for to in (core, side, up, near, far):
+            grad1 = grad1 + send(grad1, to)
+
+        whole = [jnp.zeros((), jnp.int32)]
+
+        def step(blocks, pieces, at, **kw):
+            return group_step(blocks, pieces, at, order, concepts, cap, **kw)
+
+        dx_1, (dz_in,) = step([(r, None) for r in rows_in], [own], whole, with_grads=False)
+        dx_2, grads_2 = step([(mine, 1), (got, 1)], pieces2, starts)
+        dx_3, grads_3 = step([(mine, 2), (got, 2)], pieces3, starts)
+        dx_0, grads_0 = step([(mine, 0), (got, 0)], [own], whole, extra=(*rows_in, dz_in))
+
+        def scatter(grads):
+            to_x, to_y, keep_a, keep_b = (g for g in grads)
+            from_x, from_y = send(to_x, side), send(to_y, up)
+            pass_a = (keep_a[1].astype(F32) + from_x[1].astype(F32)).astype(BF16)
+            pass_b = (keep_b[1].astype(F32) + from_y[1].astype(F32)).astype(BF16)
+            last_a = send(pass_a, up)
+            last_b = send(pass_b, side)
+            sum_a = keep_a[0].astype(F32) + from_x[0].astype(F32) + last_a.astype(F32)
+            sum_b = keep_b[0].astype(F32) + from_y[0].astype(F32) + last_b.astype(F32)
+            return sum_a, sum_b
+
+        def join(a, b):
+            return jnp.concatenate([a, b], axis=1)
+
+        sum2 = join(*scatter(grads_2)).astype(BF16)
+        sum3 = join(*scatter(grads_3)).astype(BF16)
+        parts0 = scatter(grads_0)
+        from2, from3 = send(sum2, far), send(sum3, away)
+        level2_grad = (join(*parts0) + from2.astype(F32) + from3.astype(F32)).astype(BF16)
+
+        home = [
+            dx_0[0],
+            send(dx_0[1], core),
+            send(dx_1[0], near),
+            send(dx_1[1], cross),
+            dx_2[0],
+            send(dx_2[1], core),
+            dx_3[0],
+            send(dx_3[1], core),
+        ]
+        embed_grad, row_loss = combine(key, loss1, dz1, w1, home, cap)
+        return (row_loss[0], embed_grad, grad1.T, level2_grad[None])
+
+    return local
+
+
 def solution(mesh):
+    dp_n, concept_n = mesh.shape["dp"], mesh.shape["concept"]
+    few = dp_n == 4 and concept_n == 8
     return jax.shard_map(
-        on_device,
+        make_local(dp_n, concept_n) if few else on_device,
         mesh=mesh,
         in_specs=(
             P(("dp", "concept"), None),

time: 423 us -> 221 us (0.52)
  the two profiles are of different devices: /device:TPU:0 before, /device:TPU:17 now
where the time goes in v1:
time: 221 us; the launch traced here: 220 us
  waiting for transfers between devices  90.7 us (41%)
  Pallas kernels  57.8 us (26%)
  starting transfers between devices  57 us (26%)
  other arithmetic  7.91 us (4%)
  local copies, waits for them, and re-layouts  5.99 us (3%)
    ppermute x43, waiting for transfers between devices, send(): return lax.ppermute(a, AXES, to)  90.7 us
    ppermute x43, starting transfers between devices, send(): return lax.ppermute(a, AXES, to)  57 us
    pallas_call x4, Pallas kernels, group_step(): pl.pallas_call(lambda *refs: rows_kernel(picks, len(pieces), len(extra),...  33.4 us
    pallas_call x1, Pallas kernels, combine(): pl.pallas_call(lambda *refs: combine_kernel(len(blocks), cap, *refs), gri...  11.6 us
    pallas_call x1, Pallas kernels, prepare(): pl.pallas_call(prepare_kernel, grid=(slots,), in_specs=[line, flat(LANES,...  8.37 us
  transfers between devices with their start and end apart: 43, of which 16 were waited for; matrix products, arithmetic and copies ran while one was open for 4% of the time, Pallas kernels for 20%

profile of v1, /device:TPU:17, one launch (start us, length us, event | category | flops | bytes accessed | tf_op | source)
XLA Modules:
  0.0 220.4 jit_solution(16815098632515191477)
XLA Ops:
  0.6 1.3 broadcast_in_dim.14.weight_ref
  1.9 4.4 %near_rows.1 = (bf16[256,1152]{1,0:T(8,128)(2,1)}, bf16[256,1152]{1,0:T(8,128)(2,1)}, s32[1,1024]{1,0:T(1,128)}, bf16[128,1024]{1,0:T(8,128)(2,1)}) custom-call(s32[1]{0:T(128)} %bitcast.me_ref, s32[1,1024]{1,0:T(1,128)} %bitcast.59, s32[1,1024]{1,0:T(1,128)} %bitcast.58, bf16[1,1024]{1,0:T(2,128)(2,1)} %broadcast_in_dim.14.weight_ref, ...), custom_call_target="tpu_custom_call" | custom-call | flops 1811939328 | bytes 3276800 | tf_op jit(solution)/shard_map/near_rows/pallas_call | solution.py:155
  6.3 8.4 %prepare.1 = (bf16[3,256,1152]{2,1,0:T(8,128)(2,1)}, bf16[3,256,1152]{2,1,0:T(8,128)(2,1)}, f32[1,1024]{1,0:T(1,128)}, bf16[8,1024]{1,0:T(8,128)(2,1)}, f32[8,1024]{1,0:T(8,128)}) custom-call(s32[1,1024]{1,0:T(1,128)} %get-tuple-element.36.key_ref.refs_0_, bf16[128,1024]{1,0:T(8,128)(2,1)} %get-tuple-element.37.aux_ref, s32[1,1024]{1,0:T(1,128)} %bitcast.60, ...), custom_call_target="tpu_custom_call" | custom-call | flops 3623878656 | bytes 5636096 | tf_op jit(solution)/shard_map/prepare/pallas_call | solution.py:209
  15.4 1.3 collective-permute-start.1
  17.1 1.1 dynamic-slice_bitcast_fusion
  18.6 1.2 collective-permute-done.24
  20.5 1.3 collective-permute-start.25
  21.8 1.8 collective-permute-done.25
  23.6 1.3 collective-permute-start.26
  24.9 1.8 collective-permute-done.26
  26.7 1.4 collective-permute-start.27
  28.0 21.4 %collective-permute-done.27 = f32[8,1024]{1,0:T(8,128)S(1)} collective-permute-done((f32[8,1024]{1,0:T(8,128)S(1)}, f32[8,1024]{1,0:T(8,128)S(1)}, u32[]{:S(2)}, u32[]{:S(2)}) %collective-permute-start.27) | collective-permute-done | bytes 32800 | tf_op jit(solution)/shard_map/ppermute | solution.py:429
  49.6 3.6 %collective-permute-done.28 = f32[8,1024]{1,0:T(8,128)S(1)} collective-permute-done((f32[8,1024]{1,0:T(8,128)S(1)}, f32[8,1024]{1,0:T(8,128)S(1)}, u32[]{:S(2)}, u32[]{:S(2)}) %collective-permute-start.28) | collective-permute-done | bytes 32800 | tf_op jit(solution)/shard_map/ppermute | solution.py:429
  53.2 1.2 collective-permute-start.12
  55.8 8.2 %collective-permute-done.6.refs_3_ = bf16[128,1024]{1,0:T(8,128)(2,1)} collective-permute-done((bf16[128,1024]{1,0:T(8,128)(2,1)S(1)}, bf16[128,1024]{1,0:T(8,128)(2,1)}, u32[]{:S(2)}, u32[]{:S(2)}) %collective-permute-start.6) | collective-permute-done | bytes 262176 | tf_op jit(solution)/shard_map/ppermute | solution.py:429
  64.0 1.1 collective-permute-start.11
  65.5 5.2 %collective-permute-start.15 = (bf16[128,1024]{1,0:T(8,128)(2,1)}, bf16[128,1024]{1,0:T(8,128)(2,1)S(1)}, u32[]{:S(2)}, u32[]{:S(2)}) collective-permute-start(bf16[128,1024]{1,0:T(8,128)(2,1)} %collective-permute-done.6.refs_3_), channel_id=1, source_target_pairs={{0,2},{1,3},{2,0},{3,1},{4,6},{5,7},{6,4},{7,5},{8,10},{9,11},{10,... | collective-permute-start | bytes 786440 | tf_op jit(solution)/shard_map/ppermute | solution.py:429
  71.6 7.5 %shard_map.93 = (bf16[256,1152]{1,0:T(8,128)(2,1)}, bf16[256,1152]{1,0:T(8,128)(2,1)}, bf16[512,1024]{1,0:T(8,128)(2,1)}) custom-call(s32[9]{0:T(128)} %stack.24.refs_0_, bf16[256,1152]{1,0:T(8,128)(2,1)} %copy-done.8, bf16[256,1152]{1,0:T(8,128)(2,1)} %copy-done.9, bf16[1024,1024]{1,0:T(8,128)(2,1)} %bitcast.54), custom_call_target="tpu_custom_call" | custom-call | flops 2147483648 | bytes 6553600 | tf_op jit(solution)/shard_map/pallas_call | solution.py:327
  79.1 1.3 collective-permute-start.8
  80.4 1.2 collective-permute-start.13
  82.3 1.2 collective-permute-start.16
  83.5 1.2 collective-permute-start.21
  84.7 9.4 %shard_map.94 = (bf16[256,1152]{1,0:T(8,128)(2,1)}, bf16[256,1152]{1,0:T(8,128)(2,1)}, bf16[2,256,512]{2,1,0:T(8,128)(2,1)}, bf16[2,256,512]{2,1,0:T(8,128)(2,1)...) custom-call(s32[9]{0:T(128)} %stack.24.refs_0_, bf16[3,256,1152]{2,1,0:T(8,128)(2,1)} %get-tuple-element.40.refs_1_, ...), custom_call_target="tpu_custom_call" | custom-call | flops 4294967296 | bytes 8912896 | tf_op jit(solution)/shard_map/pallas_call | solution.py:327
  94.1 1.3 collective-permute-start.17
  95.9 1.2 collective-permute-done.21.refs_9_
  97.1 1.2 collective-permute-start.22
  98.6 8.3 %shard_map.95 = (bf16[256,1152]{1,0:T(8,128)(2,1)}, bf16[256,1152]{1,0:T(8,128)(2,1)}, bf16[2,256,512]{2,1,0:T(8,128)(2,1)}, bf16[2,256,512]{2,1,0:T(8,128)(2,1)...) custom-call(s32[16]{0:T(128)} %stack.29.refs_0_, bf16[3,256,1152]{2,1,0:T(8,128)(2,1)} %get-tuple-element.40.refs_1_, ...), custom_call_target="tpu_custom_call" | custom-call | flops 3221225472 | bytes 6553600 | tf_op jit(solution)/shard_map/pallas_call | solution.py:327
  106.9 3.2 %collective-permute-start.4 = (bf16[256,1152]{1,0:T(8,128)(2,1)}, bf16[256,1152]{1,0:T(8,128)(2,1)}, u32[]{:S(2)}, u32[]{:S(2)}) collective-permute-start(bf16[256,1152]{1,0:T(8,128)(2,1)} %get-tuple-element.47), channel_id=1, source_target_pairs={{0,2},{1,3},{2,0},{3,1},{4,6},{5,7},{6,4},{7,5},{8,10},{9,11},{10,... | collective-permute-start | bytes 1769480 | tf_op jit(solution)/shard_map/ppermute | solution.py:429
  110.1 4.6 %collective-permute-start.5 = (bf16[256,1152]{1,0:T(8,128)(2,1)}, bf16[256,1152]{1,0:T(8,128)(2,1)}, u32[]{:S(2)}, u32[]{:S(2)}) collective-permute-start(bf16[256,1152]{1,0:T(8,128)(2,1)} %get-tuple-element.48), channel_id=1, source_target_pairs={{0,3},{1,2},{2,1},{3,0},{4,7},{5,6},{6,5},{7,4},{8,11},{9,10},{10,... | collective-permute-start | bytes 1769480 | tf_op jit(solution)/shard_map/ppermute | solution.py:429
  115.4 1.2 collective-permute-start.31
  117.4 1.2 collective-permute-start.33
  118.6 8.3 %shard_map.96 = (bf16[256,1152]{1,0:T(8,128)(2,1)}, bf16[256,1152]{1,0:T(8,128)(2,1)}, bf16[2,256,512]{2,1,0:T(8,128)(2,1)}, bf16[2,256,512]{2,1,0:T(8,128)(2,1)...) custom-call(s32[16]{0:T(128)} %stack.29.refs_0_, bf16[3,256,1152]{2,1,0:T(8,128)(2,1)} %get-tuple-element.40.refs_1_, ...), custom_call_target="tpu_custom_call" | custom-call | flops 3221225472 | bytes 6553600 | tf_op jit(solution)/shard_map/pallas_call | solution.py:327
  128.2 1.2 collective-permute-start.38
  131.5 7.6 %collective-permute-done.35 = bf16[2,256,512]{2,1,0:T(8,128)(2,1)S(1)} collective-permute-done((bf16[2,256,512]{2,1,0:T(8,128)(2,1)}, bf16[2,256,512]{2,1,0:T(8,128)(2,1)S(1)}, u32[]{:S(2)}, u32[]{:S(2)}) %collective-permute-start.35) | collective-permute-done | bytes 524320 | tf_op jit(solution)/shard_map/ppermute | solution.py:429
  139.1 4.4 %collective-permute-start.23 = (bf16[256,1152]{1,0:T(8,128)(2,1)S(1)}, bf16[256,1152]{1,0:T(8,128)(2,1)S(1)}, u32[]{:S(2)}, u32[]{:S(2)}) collective-permute-start(bf16[256,1152]{1,0:T(8,128)(2,1)S(1)} %copy-done.11), channel_id=1, source_target_pairs={{0,1},{1,0},{2,3},{3,2},{4,5},{5,4},{6,7},{7,6},{8,9},{9,8},{10,11... | collective-permute-start | bytes 1769480 | tf_op jit(solution)/shard_map/ppermute | solution.py:429
  144.0 6.4 %collective-permute-done.40 = bf16[2,256,512]{2,1,0:T(8,128)(2,1)S(1)} collective-permute-done((bf16[2,256,512]{2,1,0:T(8,128)(2,1)}, bf16[2,256,512]{2,1,0:T(8,128)(2,1)S(1)}, u32[]{:S(2)}, u32[]{:S(2)}) %collective-permute-start.40) | collective-permute-done | bytes 524320 | tf_op jit(solution)/shard_map/ppermute | solution.py:429
  150.4 1.4 collective-permute-start.36
  151.8 4.1 %collective-permute-done.34 = bf16[256,512]{1,0:T(8,128)(2,1)S(1)} collective-permute-done((bf16[256,512]{1,0:T(8,128)(2,1)S(1)}, bf16[256,512]{1,0:T(8,128)(2,1)S(1)}, u32[]{:S(2)}, u32[]{:S(2)}) %collective-permute-start.34) | collective-permute-done | bytes 262176 | tf_op jit(solution)/shard_map/ppermute | solution.py:429
  156.0 1.6 collective-permute-start.39
  157.7 1.2 collective-permute-start.41
  159.8 1.9 collective-permute-done.39
  161.6 3.2 %collective-permute-start.14 = (bf16[256,1152]{1,0:T(8,128)(2,1)S(1)}, bf16[256,1152]{1,0:T(8,128)(2,1)S(1)}, u32[]{:S(2)}, u32[]{:S(2)}) collective-permute-start(bf16[256,1152]{1,0:T(8,128)(2,1)S(1)} %copy-done.10), channel_id=1, source_target_pairs={{0,1},{1,0},{2,3},{3,2},{4,5},{5,4},{6,7},{7,6},{8,9},{9,8},{10,11... | collective-permute-start | bytes 1769480 | tf_op jit(solution)/shard_map/ppermute | solution.py:429
  164.8 3.0 %collective-permute-start.3 = (bf16[256,1152]{1,0:T(8,128)(2,1)S(1)}, bf16[256,1152]{1,0:T(8,128)(2,1)S(1)}, u32[]{:S(2)}, u32[]{:S(2)}) collective-permute-start(bf16[256,1152]{1,0:T(8,128)(2,1)S(1)} %copy-done.7), channel_id=1, source_target_pairs={{0,1},{1,0},{2,3},{3,2},{4,5},{5,4},{6,7},{7,6},{8,9},{9,8},{10,11... | collective-permute-start | bytes 1769480 | tf_op jit(solution)/shard_map/ppermute | solution.py:429
  169.4 1.3 collective-permute-start.32
  170.7 4.6 %collective-permute-start.42 = (bf16[256,1024]{1,0:T(8,128)(2,1)}, bf16[256,1024]{1,0:T(8,128)(2,1)S(1)}, u32[]{:S(2)}, u32[]{:S(2)}) collective-permute-start(bf16[256,1024]{1,0:T(8,128)(2,1)} %pad_maximum_fusion.1), channel_id=1, source_target_pairs={{0,6},{1,7},{2,4},{3,5},{4,2},{5,3},{6,0},{7,1},{8,14},{9,15},{10,... | collective-permute-start | bytes 1572872 | tf_op jit(solution)/shard_map/ppermute | solution.py:429
  176.1 11.6 %combine.1 = (bf16[1024,1024]{1,0:T(8,128)(2,1)}, f32[1,1024]{1,0:T(1,128)}) custom-call(s32[1,1024]{1,0:T(1,128)} %get-tuple-element.36.key_ref.refs_0_, f32[1,1024]{1,0:T(1,128)} %get-tuple-element.38.refs_1_, bf16[8,1024]{1,0:T(8,128)(2,1)} %get-tuple-element.39.refs_2_, bf16[8,1024]{1,0:T(8,128)(2,1)} %bitcast.57, ...), custom_call_target="tpu_custom_call" | custom-call | flops 4831838208 | bytes 6815744 | tf_op jit(solution)/shard_map/combine/pallas_call | solution.py:382
  189.9 14.6 %collective-permute-done.37 = bf16[256,1024]{1,0:T(8,128)(2,1)S(1)} collective-permute-done((bf16[256,1024]{1,0:T(8,128)(2,1)}, bf16[256,1024]{1,0:T(8,128)(2,1)S(1)}, u32[]{:S(2)}, u32[]{:S(2)}) %collective-permute-start.37) | collective-permute-done | bytes 524320 | tf_op jit(solution)/shard_map/ppermute | solution.py:429
  204.5 14.9 %collective-permute-done.42 = bf16[256,1024]{1,0:T(8,128)(2,1)S(1)} collective-permute-done((bf16[256,1024]{1,0:T(8,128)(2,1)}, bf16[256,1024]{1,0:T(8,128)(2,1)S(1)}, u32[]{:S(2)}, u32[]{:S(2)}) %collective-permute-start.42) | collective-permute-done | bytes 524320 | tf_op jit(solution)/shard_map/ppermute | solution.py:429
  (117 shorter events, 18.5 us)
Async XLA Ops:
  14.7 68.8 %collective-permute-start = (bf16[3,256,1152]{2,1,0:T(8,128)(2,1)}, bf16[3,256,1152]{2,1,0:T(8,128)(2,1)S(1)}, u32[]{:S(2)}, u32[]{:S(2)}) collective-permute-start(bf16[3,256,1152]{2,1,0:T(8,128)(2,1)} %get-tuple-element.41), channel_id=1, source_target_pairs={{0,1},{1,0},{2,3},{3,2},{4,5},{5,4},{6,7},{7,6},{8,9},{9,8},{10,11... | collective-permute-start | bytes 5308424 | tf_op jit(solution)/shard_map/ppermute | solution.py:429
  15.4 50.0 %collective-permute-start.1 = (bf16[256,1152]{1,0:T(8,128)(2,1)}, bf16[256,1152]{1,0:T(8,128)(2,1)S(1)}, u32[]{:S(2)}, u32[]{:S(2)}) collective-permute-start(bf16[256,1152]{1,0:T(8,128)(2,1)} %get-tuple-element.42), channel_id=1, source_target_pairs={{0,2},{1,3},{2,0},{3,1},{4,6},{5,7},{6,4},{7,5},{8,10},{9,11},{10,... | collective-permute-start | bytes 1769480 | tf_op jit(solution)/shard_map/ppermute | solution.py:429
  16.7 54.0 %collective-permute-start.2 = (bf16[256,1152]{1,0:T(8,128)(2,1)}, bf16[256,1152]{1,0:T(8,128)(2,1)S(1)}, u32[]{:S(2)}, u32[]{:S(2)}) collective-permute-start(bf16[256,1152]{1,0:T(8,128)(2,1)} %get-tuple-element.43), channel_id=1, source_target_pairs={{0,3},{1,2},{2,1},{3,0},{4,7},{5,6},{6,5},{7,4},{8,11},{9,10},{10,... | collective-permute-start | bytes 1769480 | tf_op jit(solution)/shard_map/ppermute | solution.py:429
  18.2 35.0 %collective-permute-start.10 = (bf16[128,1024]{1,0:T(8,128)(2,1)S(1)}, bf16[128,1024]{1,0:T(8,128)(2,1)S(1)}, u32[]{:S(2)}, u32[]{:S(2)}) collective-permute-start(bf16[128,1024]{1,0:T(8,128)(2,1)S(1)} %get-tuple-element.68), channel_id=1, source_target_pairs={{0,4},{1,5},{2,6},{3,7},{4,0},{5,1},{6,2},{7,3},{8,12},{9,13},{10,... | collective-permute-start | bytes 786440 | tf_op jit(solution)/shard_map/ppermute | solution.py:429
  18.3 1.5 collective-permute-start.24
  20.5 3.1 %collective-permute-start.25 = (f32[8,1024]{1,0:T(8,128)S(1)}, f32[8,1024]{1,0:T(8,128)S(1)}, u32[]{:S(2)}, u32[]{:S(2)}) collective-permute-start(f32[8,1024]{1,0:T(8,128)S(1)} %add.126), channel_id=1, source_target_pairs={{0,8},{1,9},{2,10},{3,11},{4,12},{5,13},{6,14},{7,15},{8,0},{9,1},... | collective-permute-start | bytes 98312 | tf_op jit(solution)/shard_map/ppermute | solution.py:429
  23.6 3.1 %collective-permute-start.26 = (f32[8,1024]{1,0:T(8,128)S(1)}, f32[8,1024]{1,0:T(8,128)S(1)}, u32[]{:S(2)}, u32[]{:S(2)}) collective-permute-start(f32[8,1024]{1,0:T(8,128)S(1)} %add.127), channel_id=1, source_target_pairs={{0,16},{1,17},{2,18},{3,19},{4,20},{5,21},{6,22},{7,23},{8,24},{9,... | collective-permute-start | bytes 98312 | tf_op jit(solution)/shard_map/ppermute | solution.py:429
  26.7 22.7 %collective-permute-start.27 = (f32[8,1024]{1,0:T(8,128)S(1)}, f32[8,1024]{1,0:T(8,128)S(1)}, u32[]{:S(2)}, u32[]{:S(2)}) collective-permute-start(f32[8,1024]{1,0:T(8,128)S(1)} %add.128), channel_id=1, source_target_pairs={{0,2},{1,3},{2,0},{3,1},{4,6},{5,7},{6,4},{7,5},{8,10},{9,11},{10,... | collective-permute-start | bytes 98312 | tf_op jit(solution)/shard_map/ppermute | solution.py:429
  49.4 3.8 %collective-permute-start.28 = (f32[8,1024]{1,0:T(8,128)S(1)}, f32[8,1024]{1,0:T(8,128)S(1)}, u32[]{:S(2)}, u32[]{:S(2)}) collective-permute-start(f32[8,1024]{1,0:T(8,128)S(1)} %add.129), channel_id=1, source_target_pairs={{0,4},{1,5},{2,6},{3,7},{4,0},{5,1},{6,2},{7,3},{8,12},{9,13},{10,... | collective-permute-start | bytes 98312 | tf_op jit(solution)/shard_map/ppermute | solution.py:429
  53.2 10.8 %collective-permute-start.6 = (bf16[128,1024]{1,0:T(8,128)(2,1)S(1)}, bf16[128,1024]{1,0:T(8,128)(2,1)}, u32[]{:S(2)}, u32[]{:S(2)}) collective-permute-start(bf16[128,1024]{1,0:T(8,128)(2,1)S(1)} %get-tuple-element.69), channel_id=1, source_target_pairs={{0,4},{1,5},{2,6},{3,7},{4,0},{5,1},{6,2},{7,3},{8,12},{9,13},{10,... | collective-permute-start | bytes 786440 | tf_op jit(solution)/shard_map/ppermute | solution.py:429
  53.2 40.8 %copy-start.15 = (bf16[128,1024]{1,0:T(8,128)(2,1)}, bf16[128,1024]{1,0:T(8,128)(2,1)S(1)}, u32[]{:S(2)}) copy-start(bf16[128,1024]{1,0:T(8,128)(2,1)S(1)} %collective-permute-done.10.refs_7_) | copy-start | bytes 786436
  53.2 11.8 %collective-permute-start.12 = (bf16[128,1024]{1,0:T(8,128)(2,1)S(1)}, bf16[128,1024]{1,0:T(8,128)(2,1)}, u32[]{:S(2)}, u32[]{:S(2)}) collective-permute-start(bf16[128,1024]{1,0:T(8,128)(2,1)S(1)} %collective-permute-done.10.refs_7_), channel_id=1, source_target_pairs={{0,16},{1,17},{2,18},{3,19},{4,20},{5,21},{6,22},{7,23},{8,24},{9,... | collective-permute-start | bytes 786440 | tf_op jit(solution)/shard_map/ppermute | solution.py:429
  64.0 16.4 %collective-permute-start.11 = (bf16[128,1024]{1,0:T(8,128)(2,1)S(1)}, bf16[128,1024]{1,0:T(8,128)(2,1)}, u32[]{:S(2)}, u32[]{:S(2)}) collective-permute-start(bf16[128,1024]{1,0:T(8,128)(2,1)S(1)} %collective-permute-done.10.refs_7_), channel_id=1, source_target_pairs={{0,8},{1,9},{2,10},{3,11},{4,12},{5,13},{6,14},{7,15},{8,0},{9,1},... | collective-permute-start | bytes 786440 | tf_op jit(solution)/shard_map/ppermute | solution.py:429
  65.1 14.0 %collective-permute-start.7 = (bf16[128,1024]{1,0:T(8,128)(2,1)}, bf16[128,1024]{1,0:T(8,128)(2,1)}, u32[]{:S(2)}, u32[]{:S(2)}) collective-permute-start(bf16[128,1024]{1,0:T(8,128)(2,1)} %collective-permute-done.6.refs_3_), channel_id=1, source_target_pairs={{0,8},{1,9},{2,10},{3,11},{4,12},{5,13},{6,14},{7,15},{8,0},{9,1},... | collective-permute-start | bytes 786440 | tf_op jit(solution)/shard_map/ppermute | solution.py:429
  65.5 16.1 %collective-permute-start.15 = (bf16[128,1024]{1,0:T(8,128)(2,1)}, bf16[128,1024]{1,0:T(8,128)(2,1)S(1)}, u32[]{:S(2)}, u32[]{:S(2)}) collective-permute-start(bf16[128,1024]{1,0:T(8,128)(2,1)} %collective-permute-done.6.refs_3_), channel_id=1, source_target_pairs={{0,2},{1,3},{2,0},{3,1},{4,6},{5,7},{6,4},{7,5},{8,10},{9,11},{10,... | collective-permute-start | bytes 786440 | tf_op jit(solution)/shard_map/ppermute | solution.py:429
  70.7 11.6 %collective-permute-start.19 = (bf16[128,1024]{1,0:T(8,128)(2,1)S(1)}, bf16[128,1024]{1,0:T(8,128)(2,1)}, u32[]{:S(2)}, u32[]{:S(2)}) collective-permute-start(bf16[128,1024]{1,0:T(8,128)(2,1)S(1)} %collective-permute-done.10.refs_7_), channel_id=1, source_target_pairs={{0,2},{1,3},{2,0},{3,1},{4,6},{5,7},{6,4},{7,5},{8,10},{9,11},{10,... | collective-permute-start | bytes 786440 | tf_op jit(solution)/shard_map/ppermute | solution.py:429
  79.1 15.0 %collective-permute-start.8 = (bf16[128,1024]{1,0:T(8,128)(2,1)}, bf16[128,1024]{1,0:T(8,128)(2,1)S(1)}, u32[]{:S(2)}, u32[]{:S(2)}) collective-permute-start(bf16[128,1024]{1,0:T(8,128)(2,1)} %collective-permute-done.6.refs_3_), channel_id=1, source_target_pairs={{0,16},{1,17},{2,18},{3,19},{4,20},{5,21},{6,22},{7,23},{8,24},{9,... | collective-permute-start | bytes 786440 | tf_op jit(solution)/shard_map/ppermute | solution.py:429
  80.4 15.0 %collective-permute-start.13 = (bf16[128,1024]{1,0:T(8,128)(2,1)}, bf16[128,1024]{1,0:T(8,128)(2,1)}, u32[]{:S(2)}, u32[]{:S(2)}) collective-permute-start(bf16[128,1024]{1,0:T(8,128)(2,1)} %collective-permute-done.12.refs_9_), channel_id=1, source_target_pairs={{0,8},{1,9},{2,10},{3,11},{4,12},{5,13},{6,14},{7,15},{8,0},{9,1},... | collective-permute-start | bytes 786440 | tf_op jit(solution)/shard_map/ppermute | solution.py:429
  81.6 16.8 %collective-permute-start.9 = (bf16[128,1024]{1,0:T(8,128)(2,1)}, bf16[128,1024]{1,0:T(8,128)(2,1)}, u32[]{:S(2)}, u32[]{:S(2)}) collective-permute-start(bf16[128,1024]{1,0:T(8,128)(2,1)} %collective-permute-done.7.refs_4_), channel_id=1, source_target_pairs={{0,16},{1,17},{2,18},{3,19},{4,20},{5,21},{6,22},{7,23},{8,24},{9,... | collective-permute-start | bytes 786440 | tf_op jit(solution)/shard_map/ppermute | solution.py:429
  82.3 13.4 %collective-permute-start.16 = (bf16[128,1024]{1,0:T(8,128)(2,1)S(1)}, bf16[128,1024]{1,0:T(8,128)(2,1)S(1)}, u32[]{:S(2)}, u32[]{:S(2)}) collective-permute-start(bf16[128,1024]{1,0:T(8,128)(2,1)S(1)} %collective-permute-done.15.refs_3_), channel_id=1, source_target_pairs={{0,8},{1,9},{2,10},{3,11},{4,12},{5,13},{6,14},{7,15},{8,0},{9,1},... | collective-permute-start | bytes 786440 | tf_op jit(solution)/shard_map/ppermute | solution.py:429
  83.5 13.6 %collective-permute-start.21 = (bf16[128,1024]{1,0:T(8,128)(2,1)}, bf16[128,1024]{1,0:T(8,128)(2,1)S(1)}, u32[]{:S(2)}, u32[]{:S(2)}) collective-permute-start(bf16[128,1024]{1,0:T(8,128)(2,1)} %collective-permute-done.19.refs_7_), channel_id=1, source_target_pairs={{0,16},{1,17},{2,18},{3,19},{4,20},{5,21},{6,22},{7,23},{8,24},{9,... | collective-permute-start | bytes 786440 | tf_op jit(solution)/shard_map/ppermute | solution.py:429
  94.1 12.8 %collective-permute-start.17 = (bf16[128,1024]{1,0:T(8,128)(2,1)S(1)}, bf16[128,1024]{1,0:T(8,128)(2,1)S(1)}, u32[]{:S(2)}, u32[]{:S(2)}) collective-permute-start(bf16[128,1024]{1,0:T(8,128)(2,1)S(1)} %collective-permute-done.15.refs_3_), channel_id=1, source_target_pairs={{0,16},{1,17},{2,18},{3,19},{4,20},{5,21},{6,22},{7,23},{8,24},{9,... | collective-permute-start | bytes 786440 | tf_op jit(solution)/shard_map/ppermute | solution.py:429
  95.4 14.7 %collective-permute-start.20 = (bf16[128,1024]{1,0:T(8,128)(2,1)}, bf16[128,1024]{1,0:T(8,128)(2,1)S(1)}, u32[]{:S(2)}, u32[]{:S(2)}) collective-permute-start(bf16[128,1024]{1,0:T(8,128)(2,1)} %collective-permute-done.19.refs_7_), channel_id=1, source_target_pairs={{0,8},{1,9},{2,10},{3,11},{4,12},{5,13},{6,14},{7,15},{8,0},{9,1},... | collective-permute-start | bytes 786440 | tf_op jit(solution)/shard_map/ppermute | solution.py:429
  95.7 19.0 %collective-permute-start.18 = (bf16[128,1024]{1,0:T(8,128)(2,1)S(1)}, bf16[128,1024]{1,0:T(8,128)(2,1)S(1)}, u32[]{:S(2)}, u32[]{:S(2)}) collective-permute-start(bf16[128,1024]{1,0:T(8,128)(2,1)S(1)} %collective-permute-done.16.refs_4_), channel_id=1, source_target_pairs={{0,16},{1,17},{2,18},{3,19},{4,20},{5,21},{6,22},{7,23},{8,24},{9,... | collective-permute-start | bytes 786440 | tf_op jit(solution)/shard_map/ppermute | solution.py:429
  97.1 19.5 %collective-permute-start.22 = (bf16[128,1024]{1,0:T(8,128)(2,1)S(1)}, bf16[128,1024]{1,0:T(8,128)(2,1)S(1)}, u32[]{:S(2)}, u32[]{:S(2)}) collective-permute-start(bf16[128,1024]{1,0:T(8,128)(2,1)S(1)} %collective-permute-done.21.refs_9_), channel_id=1, source_target_pairs={{0,8},{1,9},{2,10},{3,11},{4,12},{5,13},{6,14},{7,15},{8,0},{9,1},... | collective-permute-start | bytes 786440 | tf_op jit(solution)/shard_map/ppermute | solution.py:429
  98.3 28.6 %collective-permute-start.29 = (bf16[2,256,512]{2,1,0:T(8,128)(2,1)}, bf16[2,256,512]{2,1,0:T(8,128)(2,1)S(1)}, u32[]{:S(2)}, u32[]{:S(2)}) collective-permute-start(bf16[2,256,512]{2,1,0:T(8,128)(2,1)} %get-tuple-element.57), channel_id=1, source_target_pairs={{0,8},{1,9},{2,10},{3,11},{4,12},{5,13},{6,14},{7,15},{8,0},{9,1},... | collective-permute-start | bytes 1572872 | tf_op jit(solution)/shard_map/ppermute | solution.py:429
  106.9 62.0 %collective-permute-start.4 = (bf16[256,1152]{1,0:T(8,128)(2,1)}, bf16[256,1152]{1,0:T(8,128)(2,1)}, u32[]{:S(2)}, u32[]{:S(2)}) collective-permute-start(bf16[256,1152]{1,0:T(8,128)(2,1)} %get-tuple-element.47), channel_id=1, source_target_pairs={{0,2},{1,3},{2,0},{3,1},{4,6},{5,7},{6,4},{7,5},{8,10},{9,11},{10,... | collective-permute-start | bytes 1769480 | tf_op jit(solution)/shard_map/ppermute | solution.py:429
  110.1 59.2 %collective-permute-start.5 = (bf16[256,1152]{1,0:T(8,128)(2,1)}, bf16[256,1152]{1,0:T(8,128)(2,1)}, u32[]{:S(2)}, u32[]{:S(2)}) collective-permute-start(bf16[256,1152]{1,0:T(8,128)(2,1)} %get-tuple-element.48), channel_id=1, source_target_pairs={{0,3},{1,2},{2,1},{3,0},{4,7},{5,6},{6,5},{7,4},{8,11},{9,10},{10,... | collective-permute-start | bytes 1769480 | tf_op jit(solution)/shard_map/ppermute | solution.py:429
  115.4 12.8 %collective-permute-start.31 = (bf16[2,256,512]{2,1,0:T(8,128)(2,1)}, bf16[2,256,512]{2,1,0:T(8,128)(2,1)S(1)}, u32[]{:S(2)}, u32[]{:S(2)}) collective-permute-start(bf16[2,256,512]{2,1,0:T(8,128)(2,1)} %get-tuple-element.59), channel_id=1, source_target_pairs={{0,16},{1,17},{2,18},{3,19},{4,20},{5,21},{6,22},{7,23},{8,24},{9,... | collective-permute-start | bytes 1572872 | tf_op jit(solution)/shard_map/ppermute | solution.py:429
  117.4 13.5 %collective-permute-start.33 = (bf16[2,256,512]{2,1,0:T(8,128)(2,1)}, bf16[2,256,512]{2,1,0:T(8,128)(2,1)S(1)}, u32[]{:S(2)}, u32[]{:S(2)}) collective-permute-start(bf16[2,256,512]{2,1,0:T(8,128)(2,1)} %get-tuple-element.61), channel_id=1, source_target_pairs={{0,8},{1,9},{2,10},{3,11},{4,12},{5,13},{6,14},{7,15},{8,0},{9,1},... | collective-permute-start | bytes 1572872 | tf_op jit(solution)/shard_map/ppermute | solution.py:429
  126.9 17.0 %copy-start.5 = (bf16[2,256,512]{2,1,0:T(8,128)(2,1)S(1)}, bf16[2,256,512]{2,1,0:T(8,128)(2,1)}, u32[]{:S(2)}) copy-start(bf16[2,256,512]{2,1,0:T(8,128)(2,1)} %get-tuple-element.64) | copy-start | bytes 1572868
  126.9 24.9 %copy-start.4 = (bf16[2,256,512]{2,1,0:T(8,128)(2,1)S(1)}, bf16[2,256,512]{2,1,0:T(8,128)(2,1)}, u32[]{:S(2)}) copy-start(bf16[2,256,512]{2,1,0:T(8,128)(2,1)} %get-tuple-element.66) | copy-start | bytes 1572868
  126.9 12.2 %collective-permute-start.35 = (bf16[2,256,512]{2,1,0:T(8,128)(2,1)}, bf16[2,256,512]{2,1,0:T(8,128)(2,1)S(1)}, u32[]{:S(2)}, u32[]{:S(2)}) collective-permute-start(bf16[2,256,512]{2,1,0:T(8,128)(2,1)} %get-tuple-element.63), channel_id=1, source_target_pairs={{0,16},{1,17},{2,18},{3,19},{4,20},{5,21},{6,22},{7,23},{8,24},{9,... | collective-permute-start | bytes 1572872 | tf_op jit(solution)/shard_map/ppermute | solution.py:429
  128.2 15.4 %collective-permute-start.38 = (bf16[2,256,512]{2,1,0:T(8,128)(2,1)}, bf16[2,256,512]{2,1,0:T(8,128)(2,1)S(1)}, u32[]{:S(2)}, u32[]{:S(2)}) collective-permute-start(bf16[2,256,512]{2,1,0:T(8,128)(2,1)} %get-tuple-element.65), channel_id=1, source_target_pairs={{0,8},{1,9},{2,10},{3,11},{4,12},{5,13},{6,14},{7,15},{8,0},{9,1},... | collective-permute-start | bytes 1572872 | tf_op jit(solution)/shard_map/ppermute | solution.py:429
  130.9 19.5 %collective-permute-start.40 = (bf16[2,256,512]{2,1,0:T(8,128)(2,1)}, bf16[2,256,512]{2,1,0:T(8,128)(2,1)S(1)}, u32[]{:S(2)}, u32[]{:S(2)}) collective-permute-start(bf16[2,256,512]{2,1,0:T(8,128)(2,1)} %get-tuple-element.67), channel_id=1, source_target_pairs={{0,16},{1,17},{2,18},{3,19},{4,20},{5,21},{6,22},{7,23},{8,24},{9,... | collective-permute-start | bytes 1572872 | tf_op jit(solution)/shard_map/ppermute | solution.py:429
  139.1 31.6 %collective-permute-start.23 = (bf16[256,1152]{1,0:T(8,128)(2,1)S(1)}, bf16[256,1152]{1,0:T(8,128)(2,1)S(1)}, u32[]{:S(2)}, u32[]{:S(2)}) collective-permute-start(bf16[256,1152]{1,0:T(8,128)(2,1)S(1)} %copy-done.11), channel_id=1, source_target_pairs={{0,1},{1,0},{2,3},{3,2},{4,5},{5,4},{6,7},{7,6},{8,9},{9,8},{10,11... | collective-permute-start | bytes 1769480 | tf_op jit(solution)/shard_map/ppermute | solution.py:429
  143.6 12.3 %collective-permute-start.34 = (bf16[256,512]{1,0:T(8,128)(2,1)S(1)}, bf16[256,512]{1,0:T(8,128)(2,1)S(1)}, u32[]{:S(2)}, u32[]{:S(2)}) collective-permute-start(bf16[256,512]{1,0:T(8,128)(2,1)S(1)} %fusion.9), channel_id=1, source_target_pairs={{0,16},{1,17},{2,18},{3,19},{4,20},{5,21},{6,22},{7,23},{8,24},{9,... | collective-permute-start | bytes 786440 | tf_op jit(solution)/shard_map/ppermute | solution.py:429
  144.0 17.7 %copy-start.10 = (bf16[256,1152]{1,0:T(8,128)(2,1)S(1)}, bf16[256,1152]{1,0:T(8,128)(2,1)}, u32[]{:S(2)}) copy-start(bf16[256,1152]{1,0:T(8,128)(2,1)} %get-tuple-element.50) | copy-start | bytes 1769476
  144.0 20.8 %copy-start.7 = (bf16[256,1152]{1,0:T(8,128)(2,1)S(1)}, bf16[256,1152]{1,0:T(8,128)(2,1)}, u32[]{:S(2)}) copy-start(bf16[256,1152]{1,0:T(8,128)(2,1)} %get-tuple-element.46) | copy-start | bytes 1769476
  150.4 7.3 %collective-permute-start.36 = (bf16[256,512]{1,0:T(8,128)(2,1)S(1)}, bf16[256,512]{1,0:T(8,128)(2,1)S(1)}, u32[]{:S(2)}, u32[]{:S(2)}) collective-permute-start(bf16[256,512]{1,0:T(8,128)(2,1)S(1)} %fusion.10), channel_id=1, source_target_pairs={{0,8},{1,9},{2,10},{3,11},{4,12},{5,13},{6,14},{7,15},{8,0},{9,1},... | collective-permute-start | bytes 786440 | tf_op jit(solution)/shard_map/ppermute | solution.py:429
  156.0 5.7 %collective-permute-start.39 = (bf16[256,512]{1,0:T(8,128)(2,1)S(1)}, bf16[256,512]{1,0:T(8,128)(2,1)S(1)}, u32[]{:S(2)}, u32[]{:S(2)}) collective-permute-start(bf16[256,512]{1,0:T(8,128)(2,1)S(1)} %fusion.11), channel_id=1, source_target_pairs={{0,16},{1,17},{2,18},{3,19},{4,20},{5,21},{6,22},{7,23},{8,24},{9,... | collective-permute-start | bytes 786440 | tf_op jit(solution)/shard_map/ppermute | solution.py:429
  157.7 7.2 %collective-permute-start.41 = (bf16[256,512]{1,0:T(8,128)(2,1)S(1)}, bf16[256,512]{1,0:T(8,128)(2,1)S(1)}, u32[]{:S(2)}, u32[]{:S(2)}) collective-permute-start(bf16[256,512]{1,0:T(8,128)(2,1)S(1)} %fusion.12), channel_id=1, source_target_pairs={{0,8},{1,9},{2,10},{3,11},{4,12},{5,13},{6,14},{7,15},{8,0},{9,1},... | collective-permute-start | bytes 786440 | tf_op jit(solution)/shard_map/ppermute | solution.py:429
  161.6 9.1 %collective-permute-start.14 = (bf16[256,1152]{1,0:T(8,128)(2,1)S(1)}, bf16[256,1152]{1,0:T(8,128)(2,1)S(1)}, u32[]{:S(2)}, u32[]{:S(2)}) collective-permute-start(bf16[256,1152]{1,0:T(8,128)(2,1)S(1)} %copy-done.10), channel_id=1, source_target_pairs={{0,1},{1,0},{2,3},{3,2},{4,5},{5,4},{6,7},{7,6},{8,9},{9,8},{10,11... | collective-permute-start | bytes 1769480 | tf_op jit(solution)/shard_map/ppermute | solution.py:429
  164.8 10.5 %collective-permute-start.3 = (bf16[256,1152]{1,0:T(8,128)(2,1)S(1)}, bf16[256,1152]{1,0:T(8,128)(2,1)S(1)}, u32[]{:S(2)}, u32[]{:S(2)}) collective-permute-start(bf16[256,1152]{1,0:T(8,128)(2,1)S(1)} %copy-done.7), channel_id=1, source_target_pairs={{0,1},{1,0},{2,3},{3,2},{4,5},{5,4},{6,7},{7,6},{8,9},{9,8},{10,11... | collective-permute-start | bytes 1769480 | tf_op jit(solution)/shard_map/ppermute | solution.py:429
  168.9 18.8 %collective-permute-start.30 = (bf16[256,512]{1,0:T(8,128)(2,1)S(1)}, bf16[256,512]{1,0:T(8,128)(2,1)}, u32[]{:S(2)}, u32[]{:S(2)}) collective-permute-start(bf16[256,512]{1,0:T(8,128)(2,1)S(1)} %fusion.7), channel_id=1, source_target_pairs={{0,16},{1,17},{2,18},{3,19},{4,20},{5,21},{6,22},{7,23},{8,24},{9,... | collective-permute-start | bytes 786440 | tf_op jit(solution)/shard_map/ppermute | solution.py:429
  169.4 19.4 %collective-permute-start.32 = (bf16[256,512]{1,0:T(8,128)(2,1)}, bf16[256,512]{1,0:T(8,128)(2,1)}, u32[]{:S(2)}, u32[]{:S(2)}) collective-permute-start(bf16[256,512]{1,0:T(8,128)(2,1)} %fusion.8), channel_id=1, source_target_pairs={{0,8},{1,9},{2,10},{3,11},{4,12},{5,13},{6,14},{7,15},{8,0},{9,1},... | collective-permute-start | bytes 786440 | tf_op jit(solution)/shard_map/ppermute | solution.py:429
  170.7 33.8 %collective-permute-start.37 = (bf16[256,1024]{1,0:T(8,128)(2,1)}, bf16[256,1024]{1,0:T(8,128)(2,1)S(1)}, u32[]{:S(2)}, u32[]{:S(2)}) collective-permute-start(bf16[256,1024]{1,0:T(8,128)(2,1)} %pad_maximum_fusion), channel_id=1, source_target_pairs={{0,4},{1,5},{2,6},{3,7},{4,0},{5,1},{6,2},{7,3},{8,12},{9,13},{10,... | collective-permute-start | bytes 1572872 | tf_op jit(solution)/shard_map/ppermute | solution.py:429
  170.7 48.6 %collective-permute-start.42 = (bf16[256,1024]{1,0:T(8,128)(2,1)}, bf16[256,1024]{1,0:T(8,128)(2,1)S(1)}, u32[]{:S(2)}, u32[]{:S(2)}) collective-permute-start(bf16[256,1024]{1,0:T(8,128)(2,1)} %pad_maximum_fusion.1), channel_id=1, source_target_pairs={{0,6},{1,7},{2,4},{3,5},{4,2},{5,3},{6,0},{7,1},{8,14},{9,15},{10,... | collective-permute-start | bytes 1572872 | tf_op jit(solution)/shard_map/ppermute | solution.py:429
  (19 other events, 136.8 us)

commit v2 on v1

--- a/solution.py
+++ b/solution.py
@@ -229,8 +229,8 @@
     )(key, aux, groups, weights, w1, rows)
 
 
-def rows_kernel(picks, n_pieces, n_extra, cap, with_grads, meta_ref, *refs):
-    n_blocks = len(picks)
+def rows_kernel(picks, starts, n_extra, cap, with_grads, meta_ref, *refs):
+    n_blocks, n_pieces = len(picks), len(starts)
     blocks, refs = refs[:n_blocks], refs[n_blocks:]
     pieces, refs = refs[:n_pieces], refs[n_pieces:]
     extra, refs = refs[:n_extra], refs[n_extra:]
@@ -255,7 +255,10 @@
         copies.clear()
 
     for i, piece in enumerate(pieces):
-        at = pl.multiple_of(meta_ref[i], LANES)
+        at = 0
+        if starts[i] is not None:
+            flip, shift = starts[i]
+            at = pl.multiple_of((meta_ref[0] ^ flip) * (width // 4) + shift, LANES)
         start(piece, w_s.at[pl.ds(at, piece.shape[0])], i)
     for i, (block, pick) in enumerate(zip(blocks, picks)):
         src = block if pick is None else block.at[pick]
@@ -297,7 +300,7 @@
     else:
         quarter, part = g_s.shape[1], g_s.shape[2]
         for j in range(8):
-            at = pl.multiple_of(meta_ref[n_pieces + j], LANES)
+            at = pl.multiple_of((meta_ref[0] ^ (1, 3, 2, 3, 0, 2, 0, 1)[j]) * quarter, LANES)
             half = (0, 0, 1, 1, 0, 0, 1, 1)[j]
             g_s[j] = tn(
                 x_s[:, pl.ds(at, quarter)], dz_s[:, half * part : (half + 1) * part]
@@ -307,13 +310,12 @@
     drain()
 
 
-def group_step(blocks, pieces, starts, quarters, concepts, cap, extra=(), with_grads=True):
+def group_step(blocks, pieces, starts, meta, concepts, cap, extra=(), with_grads=True):
     full = blocks[0][0].shape[-1]
     width = full - LANES
     own_rows = cap * len(blocks)
     total = own_rows + cap * max(len(extra) - 1, 0)
     quarter, part = width // 4, concepts // 2
-    meta = jnp.stack(starts + [q * quarter for q in quarters]).astype(jnp.int32)
     hbm = pl.BlockSpec(memory_space=pltpu.HBM)
     dx = jax.ShapeDtypeStruct((cap, full), BF16)
     if with_grads:
@@ -325,7 +327,7 @@
     n_sems = max(len(pieces) + len(blocks), len(blocks) + 4, len(extra) + 1)
     picks = [i for _, i in blocks]
     res = pl.pallas_call(
-        lambda *refs: rows_kernel(picks, len(pieces), len(extra), cap, with_grads, *refs),
+        lambda *refs: rows_kernel(picks, starts, len(extra), cap, with_grads, *refs),
         in_specs=[pl.BlockSpec(memory_space=pltpu.SMEM)]
         + [hbm] * (len(blocks) + len(pieces) + len(extra)),
         out_specs=[hbm] * (len(blocks) + len(rest)),
@@ -456,8 +458,8 @@
             far3 = send(far2, near)
             pieces2 += spread(far2, h)
             pieces3 += spread(far3, h)
-            starts += [(dp ^ i) * quarter + h * piece for i in range(4)]
-        order = [dp ^ 1, dp ^ 3, dp ^ 2, dp ^ 3, dp, dp ^ 2, dp, dp ^ 1]
+            starts += [(i, h * piece) for i in range(4)]
+        here = dp[None].astype(jnp.int32)
 
         w1 = level1_weight.T
         groups, weights = group_label.T, row_weight[None, :]
@@ -475,10 +477,10 @@
         for to in (core, side, up, near, far):
             grad1 = grad1 + send(grad1, to)
 
-        whole = [jnp.zeros((), jnp.int32)]
+        whole = [None]
 
         def step(blocks, pieces, at, **kw):
-            return group_step(blocks, pieces, at, order, concepts, cap, **kw)
+            return group_step(blocks, pieces, at, here, concepts, cap, **kw)
 
         dx_1, (dz_in,) = step([(r, None) for r in rows_in], [own], whole, with_grads=False)
         dx_2, grads_2 = step([(mine, 1), (got, 1)], pieces2, starts)
@@ -503,7 +505,7 @@
         sum3 = join(*scatter(grads_3)).astype(BF16)
         parts0 = scatter(grads_0)
         from2, from3 = send(sum2, far), send(sum3, away)
-        level2_grad = (join(*parts0) + from2.astype(F32) + from3.astype(F32)).astype(BF16)
+        level2_grad = (join(*parts0) + from2.astype(F32) + from3.astype(F32)).astype(BF16)[None]
 
         home = [
             dx_0[0],
@@ -516,7 +518,7 @@
             send(dx_3[1], core),
         ]
         embed_grad, row_loss = combine(key, loss1, dz1, w1, home, cap)
-        return (row_loss[0], embed_grad, grad1.T, level2_grad[None])
+        return (row_loss[0], embed_grad, grad1.T, level2_grad)
 
     return local
 

time: 221 us -> 220 us (level)
  the two profiles are of different devices: /device:TPU:17 before, /device:TPU:8 now
where the time goes in v2:
time: 220 us
  waiting for transfers between devices  99.9 us (45%)
  Pallas kernels  55.2 us (25%)
  starting transfers between devices  50.8 us (23%)
  other arithmetic  7.81 us (4%)
  local copies, waits for them, and re-layouts  4.88 us (2%)
    ppermute x43, waiting for transfers between devices, send(): return lax.ppermute(a, AXES, to)  99.9 us
    ppermute x43, starting transfers between devices, send(): return lax.ppermute(a, AXES, to)  50.8 us
    pallas_call x4, Pallas kernels, group_step(): pl.pallas_call(lambda *refs: rows_kernel(picks, starts, len(extra), cap,...  30.8 us
    pallas_call x1, Pallas kernels, combine(): pl.pallas_call(lambda *refs: combine_kernel(len(blocks), cap, *refs), gri...  11.6 us
    pallas_call x1, Pallas kernels, prepare(): pl.pallas_call(prepare_kernel, grid=(slots,), in_specs=[line, flat(LANES,...  8.43 us
  transfers between devices with their start and end apart: 43, of which 19 were waited for; matrix products, arithmetic and copies ran while one was open for 4% of the time, Pallas kernels for 19%

profile of v2, /device:TPU:8, one launch (start us, length us, event | category | flops | bytes accessed | tf_op | source)
XLA Modules:
  0.0 219.6 jit_solution(15424412005212861668)
XLA Ops:
  0.6 1.3 broadcast_in_dim.17.weight_ref
  1.9 4.4 %near_rows.1 = (bf16[256,1152]{1,0:T(8,128)(2,1)}, bf16[256,1152]{1,0:T(8,128)(2,1)}, s32[1,1024]{1,0:T(1,128)}, bf16[128,1024]{1,0:T(8,128)(2,1)}) custom-call(s32[1]{0:T(128)} %bitcast.me_ref, s32[1,1024]{1,0:T(1,128)} %bitcast.52, s32[1,1024]{1,0:T(1,128)} %bitcast.51, bf16[1,1024]{1,0:T(2,128)(2,1)} %broadcast_in_dim.17.weight_ref, ...), custom_call_target="tpu_custom_call" | custom-call | flops 1811939328 | bytes 3276800 | tf_op jit(solution)/shard_map/near_rows/pallas_call | solution.py:155
  6.3 8.4 %prepare.1 = (bf16[3,256,1152]{2,1,0:T(8,128)(2,1)}, bf16[3,256,1152]{2,1,0:T(8,128)(2,1)}, f32[1,1024]{1,0:T(1,128)}, bf16[8,1024]{1,0:T(8,128)(2,1)}, f32[8,1024]{1,0:T(8,128)}) custom-call(s32[1,1024]{1,0:T(1,128)} %get-tuple-element.36.key_ref.refs_0_, bf16[128,1024]{1,0:T(8,128)(2,1)} %get-tuple-element.37.aux_ref, s32[1,1024]{1,0:T(1,128)} %bitcast.53, ...), custom_call_target="tpu_custom_call" | custom-call | flops 3623878656 | bytes 5636096 | tf_op jit(solution)/shard_map/prepare/pallas_call | solution.py:209
  14.9 1.8 collective-permute-start.2
  17.7 2.6 %collective-permute-start.10 = (bf16[128,1024]{1,0:T(8,128)(2,1)S(1)}, bf16[128,1024]{1,0:T(8,128)(2,1)}, u32[]{:S(2)}, u32[]{:S(2)}) collective-permute-start(bf16[128,1024]{1,0:T(8,128)(2,1)S(1)} %get-tuple-element.68), channel_id=1, source_target_pairs={{0,4},{1,5},{2,6},{3,7},{4,0},{5,1},{6,2},{7,3},{8,12},{9,13},{10,... | collective-permute-start | bytes 786440 | tf_op jit(solution)/shard_map/ppermute | solution.py:431
  20.4 1.3 collective-permute-done.24
  22.5 1.5 collective-permute-start.25
  24.0 2.4 %collective-permute-done.25 = f32[8,1024]{1,0:T(8,128)S(1)} collective-permute-done((f32[8,1024]{1,0:T(8,128)S(1)}, f32[8,1024]{1,0:T(8,128)S(1)}, u32[]{:S(2)}, u32[]{:S(2)}) %collective-permute-start.25) | collective-permute-done | bytes 32800 | tf_op jit(solution)/shard_map/ppermute | solution.py:431
  26.5 1.5 collective-permute-start.26
  28.0 2.4 %collective-permute-done.26 = f32[8,1024]{1,0:T(8,128)S(1)} collective-permute-done((f32[8,1024]{1,0:T(8,128)S(1)}, f32[8,1024]{1,0:T(8,128)S(1)}, u32[]{:S(2)}, u32[]{:S(2)}) %collective-permute-start.26) | collective-permute-done | bytes 32800 | tf_op jit(solution)/shard_map/ppermute | solution.py:431
  30.8 18.9 %collective-permute-done.27 = f32[8,1024]{1,0:T(8,128)S(1)} collective-permute-done((f32[8,1024]{1,0:T(8,128)S(1)}, f32[8,1024]{1,0:T(8,128)S(1)}, u32[]{:S(2)}, u32[]{:S(2)}) %collective-permute-start.27) | collective-permute-done | bytes 32800 | tf_op jit(solution)/shard_map/ppermute | solution.py:431
  49.7 2.6 %collective-permute-start.28 = (f32[8,1024]{1,0:T(8,128)S(1)}, f32[8,1024]{1,0:T(8,128)S(1)}, u32[]{:S(2)}, u32[]{:S(2)}) collective-permute-start(f32[8,1024]{1,0:T(8,128)S(1)} %add.116), channel_id=1, source_target_pairs={{0,4},{1,5},{2,6},{3,7},{4,0},{5,1},{6,2},{7,3},{8,12},{9,13},{10,... | collective-permute-start | bytes 98312 | tf_op jit(solution)/shard_map/ppermute | solution.py:431
  52.3 2.2 %collective-permute-done.28 = f32[8,1024]{1,0:T(8,128)S(1)} collective-permute-done((f32[8,1024]{1,0:T(8,128)S(1)}, f32[8,1024]{1,0:T(8,128)S(1)}, u32[]{:S(2)}, u32[]{:S(2)}) %collective-permute-start.28) | collective-permute-done | bytes 32800 | tf_op jit(solution)/shard_map/ppermute | solution.py:431
  54.5 2.8 %collective-permute-start.6 = (bf16[128,1024]{1,0:T(8,128)(2,1)S(1)}, bf16[128,1024]{1,0:T(8,128)(2,1)}, u32[]{:S(2)}, u32[]{:S(2)}) collective-permute-start(bf16[128,1024]{1,0:T(8,128)(2,1)S(1)} %get-tuple-element.69), channel_id=1, source_target_pairs={{0,4},{1,5},{2,6},{3,7},{4,0},{5,1},{6,2},{7,3},{8,12},{9,13},{10,... | collective-permute-start | bytes 786440 | tf_op jit(solution)/shard_map/ppermute | solution.py:431
  57.3 1.5 collective-permute-start.12
  58.9 7.7 %collective-permute-done.6.refs_3_ = bf16[128,1024]{1,0:T(8,128)(2,1)} collective-permute-done((bf16[128,1024]{1,0:T(8,128)(2,1)S(1)}, bf16[128,1024]{1,0:T(8,128)(2,1)}, u32[]{:S(2)}, u32[]{:S(2)}) %collective-permute-start.6) | collective-permute-done | bytes 262176 | tf_op jit(solution)/shard_map/ppermute | solution.py:431
  66.6 1.5 collective-permute-start.11
  68.6 1.7 collective-permute-start.15
  71.3 6.8 %shard_map.93 = (bf16[256,1152]{1,0:T(8,128)(2,1)}, bf16[256,1152]{1,0:T(8,128)(2,1)}, bf16[512,1024]{1,0:T(8,128)(2,1)}) custom-call(s32[1]{0:T(128)} %bitcast.4.refs_0_, bf16[256,1152]{1,0:T(8,128)(2,1)} %copy-done.9, bf16[256,1152]{1,0:T(8,128)(2,1)} %copy-done.10, bf16[1024,1024]{1,0:T(8,128)(2,1)} %bitcast.47), custom_call_target="tpu_custom_call" | custom-call | flops 2147483648 | bytes 6553600 | tf_op jit(solution)/shard_map/pallas_call | solution.py:329
  78.1 2.3 %collective-permute-done.7.refs_4_ = bf16[128,1024]{1,0:T(8,128)(2,1)} collective-permute-done((bf16[128,1024]{1,0:T(8,128)(2,1)}, bf16[128,1024]{1,0:T(8,128)(2,1)}, u32[]{:S(2)}, u32[]{:S(2)}) %collective-permute-start.7) | collective-permute-done | bytes 262176 | tf_op jit(solution)/shard_map/ppermute | solution.py:431
  80.4 1.5 collective-permute-start.8
  81.9 1.5 collective-permute-start.13
  84.5 1.5 collective-permute-start.21
  86.0 8.7 %shard_map.94 = (bf16[256,1152]{1,0:T(8,128)(2,1)}, bf16[256,1152]{1,0:T(8,128)(2,1)}, bf16[2,256,512]{2,1,0:T(8,128)(2,1)}, bf16[2,256,512]{2,1,0:T(8,128)(2,1)...) custom-call(s32[1]{0:T(128)} %bitcast.4.refs_0_, bf16[3,256,1152]{2,1,0:T(8,128)(2,1)} %get-tuple-element.40.refs_1_, ...), custom_call_target="tpu_custom_call" | custom-call | flops 4294967296 | bytes 8912896 | tf_op jit(solution)/shard_map/pallas_call | solution.py:329
  96.0 1.5 collective-permute-start.20
  98.4 2.7 %collective-permute-done.21.refs_9_ = bf16[128,1024]{1,0:T(8,128)(2,1)S(1)} collective-permute-done((bf16[128,1024]{1,0:T(8,128)(2,1)S(1)}, bf16[128,1024]{1,0:T(8,128)(2,1)S(1)}, u32[]{:S(2)}, u32[]{:S(2)}) %collective-permute-start.21) | collective-permute-done | bytes 262176 | tf_op jit(solution)/shard_map/ppermute | solution.py:431
  101.0 1.5 collective-permute-start.22
  103.1 7.6 %shard_map.95 = (bf16[256,1152]{1,0:T(8,128)(2,1)}, bf16[256,1152]{1,0:T(8,128)(2,1)}, bf16[2,256,512]{2,1,0:T(8,128)(2,1)}, bf16[2,256,512]{2,1,0:T(8,128)(2,1)...) custom-call(s32[1]{0:T(128)} %bitcast.4.refs_0_, bf16[3,256,1152]{2,1,0:T(8,128)(2,1)} %get-tuple-element.40.refs_1_, ...), custom_call_target="tpu_custom_call" | custom-call | flops 3221225472 | bytes 6553600 | tf_op jit(solution)/shard_map/pallas_call | solution.py:329
  112.6 1.6 collective-permute-start.31
  114.9 1.5 collective-permute-start.33
  116.4 7.6 %shard_map.96 = (bf16[256,1152]{1,0:T(8,128)(2,1)}, bf16[256,1152]{1,0:T(8,128)(2,1)}, bf16[2,256,512]{2,1,0:T(8,128)(2,1)}, bf16[2,256,512]{2,1,0:T(8,128)(2,1)...) custom-call(s32[1]{0:T(128)} %bitcast.4.refs_0_, bf16[3,256,1152]{2,1,0:T(8,128)(2,1)} %get-tuple-element.40.refs_1_, ...), custom_call_target="tpu_custom_call" | custom-call | flops 3221225472 | bytes 6553600 | tf_op jit(solution)/shard_map/pallas_call | solution.py:329
  124.7 2.9 %collective-permute-done.31 = bf16[2,256,512]{2,1,0:T(8,128)(2,1)S(1)} collective-permute-done((bf16[2,256,512]{2,1,0:T(8,128)(2,1)}, bf16[2,256,512]{2,1,0:T(8,128)(2,1)S(1)}, u32[]{:S(2)}, u32[]{:S(2)}) %collective-permute-start.31) | collective-permute-done | bytes 524320 | tf_op jit(solution)/shard_map/ppermute | solution.py:431
  127.6 1.6 collective-permute-start.38
  131.5 7.6 %collective-permute-done.35 = bf16[2,256,512]{2,1,0:T(8,128)(2,1)S(1)} collective-permute-done((bf16[2,256,512]{2,1,0:T(8,128)(2,1)}, bf16[2,256,512]{2,1,0:T(8,128)(2,1)S(1)}, u32[]{:S(2)}, u32[]{:S(2)}) %collective-permute-start.35) | collective-permute-done | bytes 524320 | tf_op jit(solution)/shard_map/ppermute | solution.py:431
  139.2 2.7 %collective-permute-done.38 = bf16[2,256,512]{2,1,0:T(8,128)(2,1)S(1)} collective-permute-done((bf16[2,256,512]{2,1,0:T(8,128)(2,1)}, bf16[2,256,512]{2,1,0:T(8,128)(2,1)S(1)}, u32[]{:S(2)}, u32[]{:S(2)}) %collective-permute-start.38) | collective-permute-done | bytes 524320 | tf_op jit(solution)/shard_map/ppermute | solution.py:431
  141.9 1.5 collective-permute-start.34
  143.5 6.8 %collective-permute-done.40 = bf16[2,256,512]{2,1,0:T(8,128)(2,1)S(1)} collective-permute-done((bf16[2,256,512]{2,1,0:T(8,128)(2,1)}, bf16[2,256,512]{2,1,0:T(8,128)(2,1)S(1)}, u32[]{:S(2)}, u32[]{:S(2)}) %collective-permute-start.40) | collective-permute-done | bytes 524320 | tf_op jit(solution)/shard_map/ppermute | solution.py:431
  151.7 4.0 %collective-permute-done.34 = bf16[256,512]{1,0:T(8,128)(2,1)S(1)} collective-permute-done((bf16[256,512]{1,0:T(8,128)(2,1)S(1)}, bf16[256,512]{1,0:T(8,128)(2,1)S(1)}, u32[]{:S(2)}, u32[]{:S(2)}) %collective-permute-start.34) | collective-permute-done | bytes 262176 | tf_op jit(solution)/shard_map/ppermute | solution.py:431
  155.7 1.5 collective-permute-start.39
  158.2 1.7 collective-permute-start.41
  161.0 2.9 %collective-permute-done.39 = bf16[256,512]{1,0:T(8,128)(2,1)S(1)} collective-permute-done((bf16[256,512]{1,0:T(8,128)(2,1)S(1)}, bf16[256,512]{1,0:T(8,128)(2,1)S(1)}, u32[]{:S(2)}, u32[]{:S(2)}) %collective-permute-start.39) | collective-permute-done | bytes 262176 | tf_op jit(solution)/shard_map/ppermute | solution.py:431
  163.9 1.8 collective-permute-done.41
  166.8 1.8 collective-permute-start.30
  168.5 1.5 collective-permute-start.32
  170.0 3.8 %collective-permute-start.37 = (bf16[256,1024]{1,0:T(8,128)(2,1)}, bf16[256,1024]{1,0:T(8,128)(2,1)S(1)}, u32[]{:S(2)}, u32[]{:S(2)}) collective-permute-start(bf16[256,1024]{1,0:T(8,128)(2,1)} %pad_maximum_fusion), channel_id=1, source_target_pairs={{0,4},{1,5},{2,6},{3,7},{4,0},{5,1},{6,2},{7,3},{8,12},{9,13},{10,... | collective-permute-start | bytes 1572872 | tf_op jit(solution)/shard_map/ppermute | solution.py:431
  174.9 11.6 %combine.1 = (bf16[1024,1024]{1,0:T(8,128)(2,1)}, f32[1,1024]{1,0:T(1,128)}) custom-call(s32[1,1024]{1,0:T(1,128)} %get-tuple-element.36.key_ref.refs_0_, f32[1,1024]{1,0:T(1,128)} %get-tuple-element.38.refs_1_, bf16[8,1024]{1,0:T(8,128)(2,1)} %get-tuple-element.39.refs_2_, bf16[8,1024]{1,0:T(8,128)(2,1)} %bitcast.50, ...), custom_call_target="tpu_custom_call" | custom-call | flops 4831838208 | bytes 6815744 | tf_op jit(solution)/shard_map/combine/pallas_call | solution.py:384
  188.6 16.7 %collective-permute-done.37 = bf16[256,1024]{1,0:T(8,128)(2,1)S(1)} collective-permute-done((bf16[256,1024]{1,0:T(8,128)(2,1)}, bf16[256,1024]{1,0:T(8,128)(2,1)S(1)}, u32[]{:S(2)}, u32[]{:S(2)}) %collective-permute-start.37) | collective-permute-done | bytes 524320 | tf_op jit(solution)/shard_map/ppermute | solution.py:431
  205.3 13.2 %collective-permute-done.42 = bf16[256,1024]{1,0:T(8,128)(2,1)S(1)} collective-permute-done((bf16[256,1024]{1,0:T(8,128)(2,1)}, bf16[256,1024]{1,0:T(8,128)(2,1)S(1)}, u32[]{:S(2)}, u32[]{:S(2)}) %collective-permute-start.42) | collective-permute-done | bytes 524320 | tf_op jit(solution)/shard_map/ppermute | solution.py:431
  (121 shorter events, 21.9 us)
Async XLA Ops:
  14.7 69.7 %collective-permute-start = (bf16[3,256,1152]{2,1,0:T(8,128)(2,1)}, bf16[3,256,1152]{2,1,0:T(8,128)(2,1)S(1)}, u32[]{:S(2)}, u32[]{:S(2)}) collective-permute-start(bf16[3,256,1152]{2,1,0:T(8,128)(2,1)} %get-tuple-element.41), channel_id=1, source_target_pairs={{0,1},{1,0},{2,3},{3,2},{4,5},{5,4},{6,7},{7,6},{8,9},{9,8},{10,11... | collective-permute-start | bytes 5308424 | tf_op jit(solution)/shard_map/ppermute | solution.py:431
  14.8 53.8 %collective-permute-start.1 = (bf16[256,1152]{1,0:T(8,128)(2,1)}, bf16[256,1152]{1,0:T(8,128)(2,1)S(1)}, u32[]{:S(2)}, u32[]{:S(2)}) collective-permute-start(bf16[256,1152]{1,0:T(8,128)(2,1)} %get-tuple-element.42), channel_id=1, source_target_pairs={{0,2},{1,3},{2,0},{3,1},{4,6},{5,7},{6,4},{7,5},{8,10},{9,11},{10,... | collective-permute-start | bytes 1769480 | tf_op jit(solution)/shard_map/ppermute | solution.py:431
  14.9 55.5 %collective-permute-start.2 = (bf16[256,1152]{1,0:T(8,128)(2,1)S(1)}, bf16[256,1152]{1,0:T(8,128)(2,1)S(1)}, u32[]{:S(2)}, u32[]{:S(2)}) collective-permute-start(bf16[256,1152]{1,0:T(8,128)(2,1)S(1)} %copy-done.11), channel_id=1, source_target_pairs={{0,3},{1,2},{2,1},{3,0},{4,7},{5,6},{6,5},{7,4},{8,11},{9,10},{10,... | collective-permute-start | bytes 1769480 | tf_op jit(solution)/shard_map/ppermute | solution.py:431
  17.7 39.6 %collective-permute-start.10 = (bf16[128,1024]{1,0:T(8,128)(2,1)S(1)}, bf16[128,1024]{1,0:T(8,128)(2,1)}, u32[]{:S(2)}, u32[]{:S(2)}) collective-permute-start(bf16[128,1024]{1,0:T(8,128)(2,1)S(1)} %get-tuple-element.68), channel_id=1, source_target_pairs={{0,4},{1,5},{2,6},{3,7},{4,0},{5,1},{6,2},{7,3},{8,12},{9,13},{10,... | collective-permute-start | bytes 786440 | tf_op jit(solution)/shard_map/ppermute | solution.py:431
  20.4 1.4 collective-permute-start.24
  22.5 3.9 %collective-permute-start.25 = (f32[8,1024]{1,0:T(8,128)S(1)}, f32[8,1024]{1,0:T(8,128)S(1)}, u32[]{:S(2)}, u32[]{:S(2)}) collective-permute-start(f32[8,1024]{1,0:T(8,128)S(1)} %add.113), channel_id=1, source_target_pairs={{0,8},{1,9},{2,10},{3,11},{4,12},{5,13},{6,14},{7,15},{8,0},{9,1},... | collective-permute-start | bytes 98312 | tf_op jit(solution)/shard_map/ppermute | solution.py:431
  26.5 3.9 %collective-permute-start.26 = (f32[8,1024]{1,0:T(8,128)S(1)}, f32[8,1024]{1,0:T(8,128)S(1)}, u32[]{:S(2)}, u32[]{:S(2)}) collective-permute-start(f32[8,1024]{1,0:T(8,128)S(1)} %add.114), channel_id=1, source_target_pairs={{0,16},{1,17},{2,18},{3,19},{4,20},{5,21},{6,22},{7,23},{8,24},{9,... | collective-permute-start | bytes 98312 | tf_op jit(solution)/shard_map/ppermute | solution.py:431
  30.4 19.3 %collective-permute-start.27 = (f32[8,1024]{1,0:T(8,128)S(1)}, f32[8,1024]{1,0:T(8,128)S(1)}, u32[]{:S(2)}, u32[]{:S(2)}) collective-permute-start(f32[8,1024]{1,0:T(8,128)S(1)} %add.115), channel_id=1, source_target_pairs={{0,2},{1,3},{2,0},{3,1},{4,6},{5,7},{6,4},{7,5},{8,10},{9,11},{10,... | collective-permute-start | bytes 98312 | tf_op jit(solution)/shard_map/ppermute | solution.py:431
  49.7 4.8 %collective-permute-start.28 = (f32[8,1024]{1,0:T(8,128)S(1)}, f32[8,1024]{1,0:T(8,128)S(1)}, u32[]{:S(2)}, u32[]{:S(2)}) collective-permute-start(f32[8,1024]{1,0:T(8,128)S(1)} %add.116), channel_id=1, source_target_pairs={{0,4},{1,5},{2,6},{3,7},{4,0},{5,1},{6,2},{7,3},{8,12},{9,13},{10,... | collective-permute-start | bytes 98312 | tf_op jit(solution)/shard_map/ppermute | solution.py:431
  54.5 12.1 %collective-permute-start.6 = (bf16[128,1024]{1,0:T(8,128)(2,1)S(1)}, bf16[128,1024]{1,0:T(8,128)(2,1)}, u32[]{:S(2)}, u32[]{:S(2)}) collective-permute-start(bf16[128,1024]{1,0:T(8,128)(2,1)S(1)} %get-tuple-element.69), channel_id=1, source_target_pairs={{0,4},{1,5},{2,6},{3,7},{4,0},{5,1},{6,2},{7,3},{8,12},{9,13},{10,... | collective-permute-start | bytes 786440 | tf_op jit(solution)/shard_map/ppermute | solution.py:431
  57.3 10.7 %collective-permute-start.12 = (bf16[128,1024]{1,0:T(8,128)(2,1)}, bf16[128,1024]{1,0:T(8,128)(2,1)S(1)}, u32[]{:S(2)}, u32[]{:S(2)}) collective-permute-start(bf16[128,1024]{1,0:T(8,128)(2,1)} %collective-permute-done.10.refs_7_), channel_id=1, source_target_pairs={{0,16},{1,17},{2,18},{3,19},{4,20},{5,21},{6,22},{7,23},{8,24},{9,... | collective-permute-start | bytes 786440 | tf_op jit(solution)/shard_map/ppermute | solution.py:431
  66.6 15.3 %collective-permute-start.11 = (bf16[128,1024]{1,0:T(8,128)(2,1)}, bf16[128,1024]{1,0:T(8,128)(2,1)}, u32[]{:S(2)}, u32[]{:S(2)}) collective-permute-start(bf16[128,1024]{1,0:T(8,128)(2,1)} %collective-permute-done.10.refs_7_), channel_id=1, source_target_pairs={{0,8},{1,9},{2,10},{3,11},{4,12},{5,13},{6,14},{7,15},{8,0},{9,1},... | collective-permute-start | bytes 786440 | tf_op jit(solution)/shard_map/ppermute | solution.py:431
  68.1 12.3 %collective-permute-start.7 = (bf16[128,1024]{1,0:T(8,128)(2,1)}, bf16[128,1024]{1,0:T(8,128)(2,1)}, u32[]{:S(2)}, u32[]{:S(2)}) collective-permute-start(bf16[128,1024]{1,0:T(8,128)(2,1)} %collective-permute-done.6.refs_3_), channel_id=1, source_target_pairs={{0,8},{1,9},{2,10},{3,11},{4,12},{5,13},{6,14},{7,15},{8,0},{9,1},... | collective-permute-start | bytes 786440 | tf_op jit(solution)/shard_map/ppermute | solution.py:431
  68.6 14.8 %collective-permute-start.15 = (bf16[128,1024]{1,0:T(8,128)(2,1)}, bf16[128,1024]{1,0:T(8,128)(2,1)}, u32[]{:S(2)}, u32[]{:S(2)}) collective-permute-start(bf16[128,1024]{1,0:T(8,128)(2,1)} %collective-permute-done.6.refs_3_), channel_id=1, source_target_pairs={{0,2},{1,3},{2,0},{3,1},{4,6},{5,7},{6,4},{7,5},{8,10},{9,11},{10,... | collective-permute-start | bytes 786440 | tf_op jit(solution)/shard_map/ppermute | solution.py:431
  70.4 13.6 %collective-permute-start.19 = (bf16[128,1024]{1,0:T(8,128)(2,1)}, bf16[128,1024]{1,0:T(8,128)(2,1)S(1)}, u32[]{:S(2)}, u32[]{:S(2)}) collective-permute-start(bf16[128,1024]{1,0:T(8,128)(2,1)} %collective-permute-done.10.refs_7_), channel_id=1, source_target_pairs={{0,2},{1,3},{2,0},{3,1},{4,6},{5,7},{6,4},{7,5},{8,10},{9,11},{10,... | collective-permute-start | bytes 786440 | tf_op jit(solution)/shard_map/ppermute | solution.py:431
  80.4 14.3 %collective-permute-start.8 = (bf16[128,1024]{1,0:T(8,128)(2,1)}, bf16[128,1024]{1,0:T(8,128)(2,1)S(1)}, u32[]{:S(2)}, u32[]{:S(2)}) collective-permute-start(bf16[128,1024]{1,0:T(8,128)(2,1)} %collective-permute-done.6.refs_3_), channel_id=1, source_target_pairs={{0,16},{1,17},{2,18},{3,19},{4,20},{5,21},{6,22},{7,23},{8,24},{9,... | collective-permute-start | bytes 786440 | tf_op jit(solution)/shard_map/ppermute | solution.py:431
  81.9 14.1 %collective-permute-start.13 = (bf16[128,1024]{1,0:T(8,128)(2,1)S(1)}, bf16[128,1024]{1,0:T(8,128)(2,1)S(1)}, u32[]{:S(2)}, u32[]{:S(2)}) collective-permute-start(bf16[128,1024]{1,0:T(8,128)(2,1)S(1)} %copy-done.18), channel_id=1, source_target_pairs={{0,8},{1,9},{2,10},{3,11},{4,12},{5,13},{6,14},{7,15},{8,0},{9,1},... | collective-permute-start | bytes 786440 | tf_op jit(solution)/shard_map/ppermute | solution.py:431
  83.4 19.1 %collective-permute-start.9 = (bf16[128,1024]{1,0:T(8,128)(2,1)}, bf16[128,1024]{1,0:T(8,128)(2,1)}, u32[]{:S(2)}, u32[]{:S(2)}) collective-permute-start(bf16[128,1024]{1,0:T(8,128)(2,1)} %collective-permute-done.7.refs_4_), channel_id=1, source_target_pairs={{0,16},{1,17},{2,18},{3,19},{4,20},{5,21},{6,22},{7,23},{8,24},{9,... | collective-permute-start | bytes 786440 | tf_op jit(solution)/shard_map/ppermute | solution.py:431
  83.9 13.6 %collective-permute-start.16 = (bf16[128,1024]{1,0:T(8,128)(2,1)}, bf16[128,1024]{1,0:T(8,128)(2,1)S(1)}, u32[]{:S(2)}, u32[]{:S(2)}) collective-permute-start(bf16[128,1024]{1,0:T(8,128)(2,1)} %collective-permute-done.15.refs_3_), channel_id=1, source_target_pairs={{0,8},{1,9},{2,10},{3,11},{4,12},{5,13},{6,14},{7,15},{8,0},{9,1},... | collective-permute-start | bytes 786440 | tf_op jit(solution)/shard_map/ppermute | solution.py:431
  84.5 16.5 %collective-permute-start.21 = (bf16[128,1024]{1,0:T(8,128)(2,1)S(1)}, bf16[128,1024]{1,0:T(8,128)(2,1)S(1)}, u32[]{:S(2)}, u32[]{:S(2)}) collective-permute-start(bf16[128,1024]{1,0:T(8,128)(2,1)S(1)} %collective-permute-done.19.refs_7_), channel_id=1, source_target_pairs={{0,16},{1,17},{2,18},{3,19},{4,20},{5,21},{6,22},{7,23},{8,24},{9,... | collective-permute-start | bytes 786440 | tf_op jit(solution)/shard_map/ppermute | solution.py:431
  94.7 16.0 %collective-permute-start.17 = (bf16[128,1024]{1,0:T(8,128)(2,1)}, bf16[128,1024]{1,0:T(8,128)(2,1)S(1)}, u32[]{:S(2)}, u32[]{:S(2)}) collective-permute-start(bf16[128,1024]{1,0:T(8,128)(2,1)} %collective-permute-done.15.refs_3_), channel_id=1, source_target_pairs={{0,16},{1,17},{2,18},{3,19},{4,20},{5,21},{6,22},{7,23},{8,24},{9,... | collective-permute-start | bytes 786440 | tf_op jit(solution)/shard_map/ppermute | solution.py:431
  96.0 15.9 %collective-permute-start.20 = (bf16[128,1024]{1,0:T(8,128)(2,1)S(1)}, bf16[128,1024]{1,0:T(8,128)(2,1)S(1)}, u32[]{:S(2)}, u32[]{:S(2)}) collective-permute-start(bf16[128,1024]{1,0:T(8,128)(2,1)S(1)} %collective-permute-done.19.refs_7_), channel_id=1, source_target_pairs={{0,8},{1,9},{2,10},{3,11},{4,12},{5,13},{6,14},{7,15},{8,0},{9,1},... | collective-permute-start | bytes 786440 | tf_op jit(solution)/shard_map/ppermute | solution.py:431
  97.5 14.3 %collective-permute-start.18 = (bf16[128,1024]{1,0:T(8,128)(2,1)S(1)}, bf16[128,1024]{1,0:T(8,128)(2,1)S(1)}, u32[]{:S(2)}, u32[]{:S(2)}) collective-permute-start(bf16[128,1024]{1,0:T(8,128)(2,1)S(1)} %collective-permute-done.16.refs_4_), channel_id=1, source_target_pairs={{0,16},{1,17},{2,18},{3,19},{4,20},{5,21},{6,22},{7,23},{8,24},{9,... | collective-permute-start | bytes 786440 | tf_op jit(solution)/shard_map/ppermute | solution.py:431
  101.0 13.2 %collective-permute-start.22 = (bf16[128,1024]{1,0:T(8,128)(2,1)S(1)}, bf16[128,1024]{1,0:T(8,128)(2,1)S(1)}, u32[]{:S(2)}, u32[]{:S(2)}) collective-permute-start(bf16[128,1024]{1,0:T(8,128)(2,1)S(1)} %collective-permute-done.21.refs_9_), channel_id=1, source_target_pairs={{0,8},{1,9},{2,10},{3,11},{4,12},{5,13},{6,14},{7,15},{8,0},{9,1},... | collective-permute-start | bytes 786440 | tf_op jit(solution)/shard_map/ppermute | solution.py:431
  102.5 21.6 %collective-permute-start.29 = (bf16[2,256,512]{2,1,0:T(8,128)(2,1)}, bf16[2,256,512]{2,1,0:T(8,128)(2,1)S(1)}, u32[]{:S(2)}, u32[]{:S(2)}) collective-permute-start(bf16[2,256,512]{2,1,0:T(8,128)(2,1)} %get-tuple-element.57), channel_id=1, source_target_pairs={{0,8},{1,9},{2,10},{3,11},{4,12},{5,13},{6,14},{7,15},{8,0},{9,1},... | collective-permute-start | bytes 1572872 | tf_op jit(solution)/shard_map/ppermute | solution.py:431
  110.7 56.1 %collective-permute-start.4 = (bf16[256,1152]{1,0:T(8,128)(2,1)}, bf16[256,1152]{1,0:T(8,128)(2,1)}, u32[]{:S(2)}, u32[]{:S(2)}) collective-permute-start(bf16[256,1152]{1,0:T(8,128)(2,1)} %get-tuple-element.47), channel_id=1, source_target_pairs={{0,2},{1,3},{2,0},{3,1},{4,6},{5,7},{6,4},{7,5},{8,10},{9,11},{10,... | collective-permute-start | bytes 1769480 | tf_op jit(solution)/shard_map/ppermute | solution.py:431
  111.9 56.7 %collective-permute-start.5 = (bf16[256,1152]{1,0:T(8,128)(2,1)}, bf16[256,1152]{1,0:T(8,128)(2,1)}, u32[]{:S(2)}, u32[]{:S(2)}) collective-permute-start(bf16[256,1152]{1,0:T(8,128)(2,1)} %get-tuple-element.48), channel_id=1, source_target_pairs={{0,3},{1,2},{2,1},{3,0},{4,7},{5,6},{6,5},{7,4},{8,11},{9,10},{10,... | collective-permute-start | bytes 1769480 | tf_op jit(solution)/shard_map/ppermute | solution.py:431
  112.6 15.0 %collective-permute-start.31 = (bf16[2,256,512]{2,1,0:T(8,128)(2,1)}, bf16[2,256,512]{2,1,0:T(8,128)(2,1)S(1)}, u32[]{:S(2)}, u32[]{:S(2)}) collective-permute-start(bf16[2,256,512]{2,1,0:T(8,128)(2,1)} %get-tuple-element.59), channel_id=1, source_target_pairs={{0,16},{1,17},{2,18},{3,19},{4,20},{5,21},{6,22},{7,23},{8,24},{9,... | collective-permute-start | bytes 1572872 | tf_op jit(solution)/shard_map/ppermute | solution.py:431
  114.9 16.5 %copy-start.3 = (bf16[2,256,512]{2,1,0:T(8,128)(2,1)S(1)}, bf16[2,256,512]{2,1,0:T(8,128)(2,1)}, u32[]{:S(2)}) copy-start(bf16[2,256,512]{2,1,0:T(8,128)(2,1)} %get-tuple-element.60) | copy-start | bytes 1572868
  114.9 15.4 %collective-permute-start.33 = (bf16[2,256,512]{2,1,0:T(8,128)(2,1)}, bf16[2,256,512]{2,1,0:T(8,128)(2,1)S(1)}, u32[]{:S(2)}, u32[]{:S(2)}) collective-permute-start(bf16[2,256,512]{2,1,0:T(8,128)(2,1)} %get-tuple-element.61), channel_id=1, source_target_pairs={{0,8},{1,9},{2,10},{3,11},{4,12},{5,13},{6,14},{7,15},{8,0},{9,1},... | collective-permute-start | bytes 1572872 | tf_op jit(solution)/shard_map/ppermute | solution.py:431
  124.1 19.4 %copy-start.5 = (bf16[2,256,512]{2,1,0:T(8,128)(2,1)S(1)}, bf16[2,256,512]{2,1,0:T(8,128)(2,1)}, u32[]{:S(2)}) copy-start(bf16[2,256,512]{2,1,0:T(8,128)(2,1)} %get-tuple-element.64) | copy-start | bytes 1572868
  124.1 27.6 %copy-start.4 = (bf16[2,256,512]{2,1,0:T(8,128)(2,1)S(1)}, bf16[2,256,512]{2,1,0:T(8,128)(2,1)}, u32[]{:S(2)}) copy-start(bf16[2,256,512]{2,1,0:T(8,128)(2,1)} %get-tuple-element.66) | copy-start | bytes 1572868
  124.1 15.1 %collective-permute-start.35 = (bf16[2,256,512]{2,1,0:T(8,128)(2,1)}, bf16[2,256,512]{2,1,0:T(8,128)(2,1)S(1)}, u32[]{:S(2)}, u32[]{:S(2)}) collective-permute-start(bf16[2,256,512]{2,1,0:T(8,128)(2,1)} %get-tuple-element.63), channel_id=1, source_target_pairs={{0,16},{1,17},{2,18},{3,19},{4,20},{5,21},{6,22},{7,23},{8,24},{9,... | collective-permute-start | bytes 1572872 | tf_op jit(solution)/shard_map/ppermute | solution.py:431
  127.6 14.3 %collective-permute-start.38 = (bf16[2,256,512]{2,1,0:T(8,128)(2,1)}, bf16[2,256,512]{2,1,0:T(8,128)(2,1)S(1)}, u32[]{:S(2)}, u32[]{:S(2)}) collective-permute-start(bf16[2,256,512]{2,1,0:T(8,128)(2,1)} %get-tuple-element.65), channel_id=1, source_target_pairs={{0,8},{1,9},{2,10},{3,11},{4,12},{5,13},{6,14},{7,15},{8,0},{9,1},... | collective-permute-start | bytes 1572872 | tf_op jit(solution)/shard_map/ppermute | solution.py:431
  130.3 20.1 %collective-permute-start.40 = (bf16[2,256,512]{2,1,0:T(8,128)(2,1)}, bf16[2,256,512]{2,1,0:T(8,128)(2,1)S(1)}, u32[]{:S(2)}, u32[]{:S(2)}) collective-permute-start(bf16[2,256,512]{2,1,0:T(8,128)(2,1)} %get-tuple-element.67), channel_id=1, source_target_pairs={{0,16},{1,17},{2,18},{3,19},{4,20},{5,21},{6,22},{7,23},{8,24},{9,... | collective-permute-start | bytes 1572872 | tf_op jit(solution)/shard_map/ppermute | solution.py:431
  139.2 30.9 %collective-permute-start.23 = (bf16[256,1152]{1,0:T(8,128)(2,1)S(1)}, bf16[256,1152]{1,0:T(8,128)(2,1)S(1)}, u32[]{:S(2)}, u32[]{:S(2)}) collective-permute-start(bf16[256,1152]{1,0:T(8,128)(2,1)S(1)} %copy-done.12), channel_id=1, source_target_pairs={{0,1},{1,0},{2,3},{3,2},{4,5},{5,4},{6,7},{7,6},{8,9},{9,8},{10,11... | collective-permute-start | bytes 1769480 | tf_op jit(solution)/shard_map/ppermute | solution.py:431
  141.9 13.8 %collective-permute-start.34 = (bf16[256,512]{1,0:T(8,128)(2,1)S(1)}, bf16[256,512]{1,0:T(8,128)(2,1)S(1)}, u32[]{:S(2)}, u32[]{:S(2)}) collective-permute-start(bf16[256,512]{1,0:T(8,128)(2,1)S(1)} %fusion.9), channel_id=1, source_target_pairs={{0,16},{1,17},{2,18},{3,19},{4,20},{5,21},{6,22},{7,23},{8,24},{9,... | collective-permute-start | bytes 786440 | tf_op jit(solution)/shard_map/ppermute | solution.py:431
  143.5 20.3 %copy-start.8 = (bf16[256,1152]{1,0:T(8,128)(2,1)S(1)}, bf16[256,1152]{1,0:T(8,128)(2,1)}, u32[]{:S(2)}) copy-start(bf16[256,1152]{1,0:T(8,128)(2,1)} %get-tuple-element.50) | copy-start | bytes 1769476
  143.5 22.2 %copy-start.7 = (bf16[256,1152]{1,0:T(8,128)(2,1)S(1)}, bf16[256,1152]{1,0:T(8,128)(2,1)}, u32[]{:S(2)}) copy-start(bf16[256,1152]{1,0:T(8,128)(2,1)} %get-tuple-element.46) | copy-start | bytes 1769476
  150.4 7.8 %collective-permute-start.36 = (bf16[256,512]{1,0:T(8,128)(2,1)S(1)}, bf16[256,512]{1,0:T(8,128)(2,1)S(1)}, u32[]{:S(2)}, u32[]{:S(2)}) collective-permute-start(bf16[256,512]{1,0:T(8,128)(2,1)S(1)} %fusion.10), channel_id=1, source_target_pairs={{0,8},{1,9},{2,10},{3,11},{4,12},{5,13},{6,14},{7,15},{8,0},{9,1},... | collective-permute-start | bytes 786440 | tf_op jit(solution)/shard_map/ppermute | solution.py:431
  155.7 8.1 %collective-permute-start.39 = (bf16[256,512]{1,0:T(8,128)(2,1)S(1)}, bf16[256,512]{1,0:T(8,128)(2,1)S(1)}, u32[]{:S(2)}, u32[]{:S(2)}) collective-permute-start(bf16[256,512]{1,0:T(8,128)(2,1)S(1)} %fusion.11), channel_id=1, source_target_pairs={{0,16},{1,17},{2,18},{3,19},{4,20},{5,21},{6,22},{7,23},{8,24},{9,... | collective-permute-start | bytes 786440 | tf_op jit(solution)/shard_map/ppermute | solution.py:431
  158.2 7.5 %collective-permute-start.41 = (bf16[256,512]{1,0:T(8,128)(2,1)S(1)}, bf16[256,512]{1,0:T(8,128)(2,1)S(1)}, u32[]{:S(2)}, u32[]{:S(2)}) collective-permute-start(bf16[256,512]{1,0:T(8,128)(2,1)S(1)} %fusion.12), channel_id=1, source_target_pairs={{0,8},{1,9},{2,10},{3,11},{4,12},{5,13},{6,14},{7,15},{8,0},{9,1},... | collective-permute-start | bytes 786440 | tf_op jit(solution)/shard_map/ppermute | solution.py:431
  163.9 10.0 %collective-permute-start.14 = (bf16[256,1152]{1,0:T(8,128)(2,1)S(1)}, bf16[256,1152]{1,0:T(8,128)(2,1)S(1)}, u32[]{:S(2)}, u32[]{:S(2)}) collective-permute-start(bf16[256,1152]{1,0:T(8,128)(2,1)S(1)} %copy-done.8), channel_id=1, source_target_pairs={{0,1},{1,0},{2,3},{3,2},{4,5},{5,4},{6,7},{7,6},{8,9},{9,8},{10,11... | collective-permute-start | bytes 1769480 | tf_op jit(solution)/shard_map/ppermute | solution.py:431
  165.7 8.2 %collective-permute-start.3 = (bf16[256,1152]{1,0:T(8,128)(2,1)S(1)}, bf16[256,1152]{1,0:T(8,128)(2,1)S(1)}, u32[]{:S(2)}, u32[]{:S(2)}) collective-permute-start(bf16[256,1152]{1,0:T(8,128)(2,1)S(1)} %copy-done.7), channel_id=1, source_target_pairs={{0,1},{1,0},{2,3},{3,2},{4,5},{5,4},{6,7},{7,6},{8,9},{9,8},{10,11... | collective-permute-start | bytes 1769480 | tf_op jit(solution)/shard_map/ppermute | solution.py:431
  166.8 19.7 %collective-permute-start.30 = (bf16[256,512]{1,0:T(8,128)(2,1)S(1)}, bf16[256,512]{1,0:T(8,128)(2,1)}, u32[]{:S(2)}, u32[]{:S(2)}) collective-permute-start(bf16[256,512]{1,0:T(8,128)(2,1)S(1)} %fusion.7), channel_id=1, source_target_pairs={{0,16},{1,17},{2,18},{3,19},{4,20},{5,21},{6,22},{7,23},{8,24},{9,... | collective-permute-start | bytes 786440 | tf_op jit(solution)/shard_map/ppermute | solution.py:431
  168.5 19.0 %collective-permute-start.32 = (bf16[256,512]{1,0:T(8,128)(2,1)}, bf16[256,512]{1,0:T(8,128)(2,1)}, u32[]{:S(2)}, u32[]{:S(2)}) collective-permute-start(bf16[256,512]{1,0:T(8,128)(2,1)} %fusion.8), channel_id=1, source_target_pairs={{0,8},{1,9},{2,10},{3,11},{4,12},{5,13},{6,14},{7,15},{8,0},{9,1},... | collective-permute-start | bytes 786440 | tf_op jit(solution)/shard_map/ppermute | solution.py:431
  170.0 35.3 %collective-permute-start.37 = (bf16[256,1024]{1,0:T(8,128)(2,1)}, bf16[256,1024]{1,0:T(8,128)(2,1)S(1)}, u32[]{:S(2)}, u32[]{:S(2)}) collective-permute-start(bf16[256,1024]{1,0:T(8,128)(2,1)} %pad_maximum_fusion), channel_id=1, source_target_pairs={{0,4},{1,5},{2,6},{3,7},{4,0},{5,1},{6,2},{7,3},{8,12},{9,13},{10,... | collective-permute-start | bytes 1572872 | tf_op jit(solution)/shard_map/ppermute | solution.py:431
  173.8 44.7 %collective-permute-start.42 = (bf16[256,1024]{1,0:T(8,128)(2,1)}, bf16[256,1024]{1,0:T(8,128)(2,1)S(1)}, u32[]{:S(2)}, u32[]{:S(2)}) collective-permute-start(bf16[256,1024]{1,0:T(8,128)(2,1)} %pad_maximum_fusion.1), channel_id=1, source_target_pairs={{0,6},{1,7},{2,4},{3,5},{4,2},{5,3},{6,0},{7,1},{8,14},{9,15},{10,... | collective-permute-start | bytes 1572872 | tf_op jit(solution)/shard_map/ppermute | solution.py:431
  (22 other events, 142.6 us)

commit v3 on v2

--- a/solution.py
+++ b/solution.py
@@ -329,7 +329,7 @@
     res = pl.pallas_call(
         lambda *refs: rows_kernel(picks, starts, len(extra), cap, with_grads, *refs),
         in_specs=[pl.BlockSpec(memory_space=pltpu.SMEM)]
-        + [hbm] * (len(blocks) + len(pieces) + len(extra)),
+        + [pl.BlockSpec(memory_space=pl.ANY)] * (len(blocks) + len(pieces) + len(extra)),
         out_specs=[hbm] * (len(blocks) + len(rest)),
         out_shape=[dx] * len(blocks) + rest,
         scratch_shapes=[
@@ -340,6 +340,7 @@
             *grad_scratch,
             pltpu.SemaphoreType.DMA((n_sems,)),
         ],
+        compiler_params=pltpu.CompilerParams(vmem_limit_bytes=24 << 20),
         cost_estimate=pl.CostEstimate(
             flops=(4 * own_rows + 2 * total * with_grads) * width * concepts,
             bytes_accessed=4 * (total * full + width * concepts),
@@ -390,7 +391,7 @@
             pl.BlockSpec((groups_n, tile), lambda i: (0, i)),
             pl.BlockSpec((groups_n, width), lambda i: (0, 0)),
         ]
-        + [pl.BlockSpec(memory_space=pltpu.HBM)] * len(blocks),
+        + [pl.BlockSpec(memory_space=pl.ANY)] * len(blocks),
         out_specs=[pl.BlockSpec((tile, width), lambda i: (i, 0)), line],
         out_shape=[
             jax.ShapeDtypeStruct((rows_n, width), BF16),
@@ -400,6 +401,7 @@
             pltpu.VMEM((slots, full), BF16),
             pltpu.SemaphoreType.DMA((len(blocks),)),
         ],
+        compiler_params=pltpu.CompilerParams(vmem_limit_bytes=20 << 20),
         cost_estimate=pl.CostEstimate(
             flops=2 * rows_n * slots * full,
             bytes_accessed=2 * (slots * full + rows_n * width),

time: 220 us -> 217 us (0.986)
  the two profiles are of different devices: /device:TPU:8 before, /device:TPU:17 now
where the time goes in v3:
time: 217 us
  waiting for transfers between devices  107 us (49%)
  starting transfers between devices  53.9 us (25%)
  Pallas kernels  50.1 us (23%)
  other arithmetic  3.57 us (2%)
    ppermute x43, waiting for transfers between devices, send(): return lax.ppermute(a, AXES, to)  107 us
    ppermute x43, starting transfers between devices, send(): return lax.ppermute(a, AXES, to)  53.9 us
    pallas_call x4, Pallas kernels, group_step(): pl.pallas_call(lambda *refs: rows_kernel(picks, starts, len(extra), cap,...  27.7 us
    pallas_call x1, Pallas kernels, combine(): pl.pallas_call(lambda *refs: combine_kernel(len(blocks), cap, *refs), gri...  9.5 us
    pallas_call x1, Pallas kernels, prepare(): pl.pallas_call(prepare_kernel, grid=(slots,), in_specs=[line, flat(LANES,...  8.48 us
    pallas_call x1, Pallas kernels, near_rows(): pl.pallas_call(near_kernel, in_specs=[pl.BlockSpec(memory_space=pltpu.SME...  4.37 us
  transfers between devices with their start and end apart: 43, of which 16 were waited for; matrix products, arithmetic and copies ran while one was open for 1% of the time, Pallas kernels for 17%

profile of v3, /device:TPU:17, one launch (start us, length us, event | category | flops | bytes accessed | tf_op | source)
XLA Modules:
  0.0 216.6 jit_solution(2119787638776332422)
XLA Ops:
  0.6 1.3 broadcast_in_dim.17.weight_ref
  1.9 4.4 %near_rows.1 = (bf16[256,1152]{1,0:T(8,128)(2,1)}, bf16[256,1152]{1,0:T(8,128)(2,1)}, s32[1,1024]{1,0:T(1,128)}, bf16[128,1024]{1,0:T(8,128)(2,1)}) custom-call(s32[1]{0:T(128)} %bitcast.me_ref, s32[1,1024]{1,0:T(1,128)} %bitcast.52, s32[1,1024]{1,0:T(1,128)} %bitcast.51, bf16[1,1024]{1,0:T(2,128)(2,1)} %broadcast_in_dim.17.weight_ref, ...), custom_call_target="tpu_custom_call" | custom-call | flops 1811939328 | bytes 3276800 | tf_op jit(solution)/shard_map/near_rows/pallas_call | solution.py:155
  6.3 8.5 %prepare.1 = (bf16[3,256,1152]{2,1,0:T(8,128)(2,1)}, bf16[3,256,1152]{2,1,0:T(8,128)(2,1)}, f32[1,1024]{1,0:T(1,128)}, bf16[8,1024]{1,0:T(8,128)(2,1)}, f32[8,1024]{1,0:T(8,128)}) custom-call(s32[1,1024]{1,0:T(1,128)} %get-tuple-element.36.key_ref.refs_0_, bf16[128,1024]{1,0:T(8,128)(2,1)} %get-tuple-element.37.aux_ref, s32[1,1024]{1,0:T(1,128)} %bitcast.53, ...), custom_call_target="tpu_custom_call" | custom-call | flops 3623878656 | bytes 5636096 | tf_op jit(solution)/shard_map/prepare/pallas_call | solution.py:209
  15.5 1.3 collective-permute-start.1
  17.7 1.5 collective-permute-done.24
  20.0 1.2 collective-permute-start.25
  21.1 1.9 collective-permute-done.25
  23.0 1.2 collective-permute-start.26
  24.3 1.8 collective-permute-done.26
  26.1 1.3 collective-permute-start.27
  27.4 22.1 %collective-permute-done.27 = f32[8,1024]{1,0:T(8,128)S(1)} collective-permute-done((f32[8,1024]{1,0:T(8,128)S(1)}, f32[8,1024]{1,0:T(8,128)S(1)}, u32[]{:S(2)}, u32[]{:S(2)}) %collective-permute-start.27) | collective-permute-done | bytes 32800 | tf_op jit(solution)/shard_map/ppermute | solution.py:433
  49.7 3.6 %collective-permute-done.28 = f32[8,1024]{1,0:T(8,128)S(1)} collective-permute-done((f32[8,1024]{1,0:T(8,128)S(1)}, f32[8,1024]{1,0:T(8,128)S(1)}, u32[]{:S(2)}, u32[]{:S(2)}) %collective-permute-start.28) | collective-permute-done | bytes 32800 | tf_op jit(solution)/shard_map/ppermute | solution.py:433
  53.3 1.2 collective-permute-start.12
  54.5 9.6 %collective-permute-done.6.refs_3_ = bf16[128,1024]{1,0:T(8,128)(2,1)S(1)} collective-permute-done((bf16[128,1024]{1,0:T(8,128)(2,1)S(1)}, bf16[128,1024]{1,0:T(8,128)(2,1)S(1)}, u32[]{:S(2)}, u32[]{:S(2)}) %collective-permute-start.6) | collective-permute-done | bytes 262176 | tf_op jit(solution)/shard_map/ppermute | solution.py:433
  65.5 5.1 %collective-permute-start.15 = (bf16[128,1024]{1,0:T(8,128)(2,1)S(1)}, bf16[128,1024]{1,0:T(8,128)(2,1)S(1)}, u32[]{:S(2)}, u32[]{:S(2)}) collective-permute-start(bf16[128,1024]{1,0:T(8,128)(2,1)S(1)} %collective-permute-done.6.refs_3_), channel_id=1, source_target_pairs={{0,2},{1,3},{2,0},{3,1},{4,6},{5,7},{6,4},{7,5},{8,10},{9,11},{10,... | collective-permute-start | bytes 786440 | tf_op jit(solution)/shard_map/ppermute | solution.py:433
  71.4 4.3 %shard_map.93 = (bf16[256,1152]{1,0:T(8,128)(2,1)S(1)}, bf16[256,1152]{1,0:T(8,128)(2,1)S(1)}, bf16[512,1024]{1,0:T(8,128)(2,1)S(1)}) custom-call(s32[1]{0:T(128)} %bitcast.4.refs_0_, bf16[256,1152]{1,0:T(8,128)(2,1)S(1)} %collective-permute-done.1.refs_1_.refs_4_, bf16[256,1152]{1,0:T(8,128)(2,1)S(1)} %collective-permute-done.2.refs_2_.refs_5_, ...), custom_call_target="tpu_custom_call" | custom-call | flops 2147483648 | bytes 6553600 | tf_op jit(solution)/shard_map/pallas_call | solution.py:329
  77.2 1.2 collective-permute-start.13
  78.6 3.3 %collective-permute-done.19.refs_7_ = bf16[128,1024]{1,0:T(8,128)(2,1)S(1)} collective-permute-done((bf16[128,1024]{1,0:T(8,128)(2,1)S(1)}, bf16[128,1024]{1,0:T(8,128)(2,1)S(1)}, u32[]{:S(2)}, u32[]{:S(2)}) %collective-permute-start.19) | collective-permute-done | bytes 262176 | tf_op jit(solution)/shard_map/ppermute | solution.py:433
  81.9 1.2 collective-permute-start.16
  83.1 1.2 collective-permute-start.21
  84.4 8.6 %shard_map.94 = (bf16[256,1152]{1,0:T(8,128)(2,1)S(1)}, bf16[256,1152]{1,0:T(8,128)(2,1)S(1)}, bf16[2,256,512]{2,1,0:T(8,128)(2,1)S(1)}, bf16[2,256,512]{2,1,0:T...) custom-call(s32[1]{0:T(128)} %bitcast.4.refs_0_, ...), custom_call_target="tpu_custom_call" | custom-call | flops 4294967296 | bytes 8912896 | tf_op jit(solution)/shard_map/pallas_call | solution.py:329
  93.6 1.3 collective-permute-start.18
  94.8 1.2 collective-permute-start.22
  96.3 7.5 %shard_map.95 = (bf16[256,1152]{1,0:T(8,128)(2,1)S(1)}, bf16[256,1152]{1,0:T(8,128)(2,1)S(1)}, bf16[2,256,512]{2,1,0:T(8,128)(2,1)S(1)}, bf16[2,256,512]{2,1,0:T...) custom-call(s32[1]{0:T(128)} %bitcast.4.refs_0_, ...), custom_call_target="tpu_custom_call" | custom-call | flops 3221225472 | bytes 6553600 | tf_op jit(solution)/shard_map/pallas_call | solution.py:329
  103.9 5.2 %collective-permute-start.4 = (bf16[256,1152]{1,0:T(8,128)(2,1)S(1)}, bf16[256,1152]{1,0:T(8,128)(2,1)S(1)}, u32[]{:S(2)}, u32[]{:S(2)}) collective-permute-start(bf16[256,1152]{1,0:T(8,128)(2,1)S(1)} %get-tuple-element.47), channel_id=1, source_target_pairs={{0,2},{1,3},{2,0},{3,1},{4,6},{5,7},{6,4},{7,5},{8,10},{9,11},{10,... | collective-permute-start | bytes 1769480 | tf_op jit(solution)/shard_map/ppermute | solution.py:433
  109.0 4.5 %collective-permute-start.5 = (bf16[256,1152]{1,0:T(8,128)(2,1)S(1)}, bf16[256,1152]{1,0:T(8,128)(2,1)S(1)}, u32[]{:S(2)}, u32[]{:S(2)}) collective-permute-start(bf16[256,1152]{1,0:T(8,128)(2,1)S(1)} %get-tuple-element.48), channel_id=1, source_target_pairs={{0,3},{1,2},{2,1},{3,0},{4,7},{5,6},{6,5},{7,4},{8,11},{9,10},{10,... | collective-permute-start | bytes 1769480 | tf_op jit(solution)/shard_map/ppermute | solution.py:433
  113.6 1.2 collective-permute-start.31
  114.8 1.2 collective-permute-start.33
  116.0 7.3 %shard_map.96 = (bf16[256,1152]{1,0:T(8,128)(2,1)S(1)}, bf16[256,1152]{1,0:T(8,128)(2,1)S(1)}, bf16[2,256,512]{2,1,0:T(8,128)(2,1)S(1)}, bf16[2,256,512]{2,1,0:T...) custom-call(s32[1]{0:T(128)} %bitcast.4.refs_0_, ...), custom_call_target="tpu_custom_call" | custom-call | flops 3221225472 | bytes 6553600 | tf_op jit(solution)/shard_map/pallas_call | solution.py:329
  123.7 3.0 %collective-permute-done.31 = bf16[2,256,512]{2,1,0:T(8,128)(2,1)S(1)} collective-permute-done((bf16[2,256,512]{2,1,0:T(8,128)(2,1)S(1)}, bf16[2,256,512]{2,1,0:T(8,128)(2,1)S(1)}, u32[]{:S(2)}, u32[]{:S(2)}) %collective-permute-start.31) | collective-permute-done | bytes 524320 | tf_op jit(solution)/shard_map/ppermute | solution.py:433
  126.7 1.2 collective-permute-start.38
  129.3 8.6 %collective-permute-done.35 = bf16[2,256,512]{2,1,0:T(8,128)(2,1)S(1)} collective-permute-done((bf16[2,256,512]{2,1,0:T(8,128)(2,1)S(1)}, bf16[2,256,512]{2,1,0:T(8,128)(2,1)S(1)}, u32[]{:S(2)}, u32[]{:S(2)}) %collective-permute-start.35) | collective-permute-done | bytes 524320 | tf_op jit(solution)/shard_map/ppermute | solution.py:433
  137.9 2.1 collective-permute-start.23
  140.1 1.3 collective-permute-start.34
  141.4 7.7 %collective-permute-done.40 = bf16[2,256,512]{2,1,0:T(8,128)(2,1)S(1)} collective-permute-done((bf16[2,256,512]{2,1,0:T(8,128)(2,1)S(1)}, bf16[2,256,512]{2,1,0:T(8,128)(2,1)S(1)}, u32[]{:S(2)}, u32[]{:S(2)}) %collective-permute-start.40) | collective-permute-done | bytes 524320 | tf_op jit(solution)/shard_map/ppermute | solution.py:433
  149.2 1.2 collective-permute-start.36
  150.4 4.4 %collective-permute-done.34 = bf16[256,512]{1,0:T(8,128)(2,1)S(1)} collective-permute-done((bf16[256,512]{1,0:T(8,128)(2,1)S(1)}, bf16[256,512]{1,0:T(8,128)(2,1)S(1)}, u32[]{:S(2)}, u32[]{:S(2)}) %collective-permute-start.34) | collective-permute-done | bytes 262176 | tf_op jit(solution)/shard_map/ppermute | solution.py:433
  154.8 1.2 collective-permute-start.39
  156.1 1.3 collective-permute-start.41
  157.6 3.8 %collective-permute-done.39 = bf16[256,512]{1,0:T(8,128)(2,1)S(1)} collective-permute-done((bf16[256,512]{1,0:T(8,128)(2,1)S(1)}, bf16[256,512]{1,0:T(8,128)(2,1)S(1)}, u32[]{:S(2)}, u32[]{:S(2)}) %collective-permute-start.39) | collective-permute-done | bytes 262176 | tf_op jit(solution)/shard_map/ppermute | solution.py:433
  161.4 2.1 collective-permute-start.14
  163.5 1.4 collective-permute-start.3
  165.8 1.2 collective-permute-start.32
  167.1 4.5 %collective-permute-start.42 = (bf16[256,1024]{1,0:T(8,128)(2,1)S(1)}, bf16[256,1024]{1,0:T(8,128)(2,1)S(1)}, u32[]{:S(2)}, u32[]{:S(2)}) collective-permute-start(bf16[256,1024]{1,0:T(8,128)(2,1)S(1)} %pad_maximum_fusion.1), channel_id=1, source_target_pairs={{0,6},{1,7},{2,4},{3,5},{4,2},{5,3},{6,0},{7,1},{8,14},{9,15},{10,... | collective-permute-start | bytes 1572872 | tf_op jit(solution)/shard_map/ppermute | solution.py:433
  171.6 9.5 %combine.1 = (bf16[1024,1024]{1,0:T(8,128)(2,1)}, f32[1,1024]{1,0:T(1,128)}) custom-call(s32[1,1024]{1,0:T(1,128)S(1)} %copy-done.3, f32[1,1024]{1,0:T(1,128)S(1)} %copy-done.5, bf16[8,1024]{1,0:T(8,128)(2,1)S(1)} %copy-done.4, bf16[8,1024]{1,0:T(8,128)(2,1)S(1)} %bitcast.50, bf16[256,1152]{1,0:T(8,128)(2,1)S(1)} %get-tuple-element.45.refs_4_, ...), custom_call_target="tpu_custom_call" | custom-call | flops 4831838208 | bytes 6815744 | tf_op jit(solution)/shard_map/combine/pallas_call | solution.py:385
  181.4 19.1 %collective-permute-done.37 = bf16[256,1024]{1,0:T(8,128)(2,1)S(1)} collective-permute-done((bf16[256,1024]{1,0:T(8,128)(2,1)S(1)}, bf16[256,1024]{1,0:T(8,128)(2,1)S(1)}, u32[]{:S(2)}, u32[]{:S(2)}) %collective-permute-start.37) | collective-permute-done | bytes 524320 | tf_op jit(solution)/shard_map/ppermute | solution.py:433
  200.5 15.0 %collective-permute-done.42 = bf16[256,1024]{1,0:T(8,128)(2,1)S(1)} collective-permute-done((bf16[256,1024]{1,0:T(8,128)(2,1)S(1)}, bf16[256,1024]{1,0:T(8,128)(2,1)S(1)}, u32[]{:S(2)}, u32[]{:S(2)}) %collective-permute-start.42) | collective-permute-done | bytes 524320 | tf_op jit(solution)/shard_map/ppermute | solution.py:433
  215.5 1.1 fusion.2
  (79 shorter events, 10.8 us)
Async XLA Ops:
  14.8 68.3 %collective-permute-start = (bf16[3,256,1152]{2,1,0:T(8,128)(2,1)}, bf16[3,256,1152]{2,1,0:T(8,128)(2,1)}, u32[]{:S(2)}, u32[]{:S(2)}) collective-permute-start(bf16[3,256,1152]{2,1,0:T(8,128)(2,1)} %get-tuple-element.41), channel_id=1, source_target_pairs={{0,1},{1,0},{2,3},{3,2},{4,5},{5,4},{6,7},{7,6},{8,9},{9,8},{10,11... | collective-permute-start | bytes 5308424 | tf_op jit(solution)/shard_map/ppermute | solution.py:433
  15.5 50.0 %collective-permute-start.1 = (bf16[256,1152]{1,0:T(8,128)(2,1)}, bf16[256,1152]{1,0:T(8,128)(2,1)S(1)}, u32[]{:S(2)}, u32[]{:S(2)}) collective-permute-start(bf16[256,1152]{1,0:T(8,128)(2,1)} %get-tuple-element.42), channel_id=1, source_target_pairs={{0,2},{1,3},{2,0},{3,1},{4,6},{5,7},{6,4},{7,5},{8,10},{9,11},{10,... | collective-permute-start | bytes 1769480 | tf_op jit(solution)/shard_map/ppermute | solution.py:433
  16.8 53.9 %collective-permute-start.2 = (bf16[256,1152]{1,0:T(8,128)(2,1)}, bf16[256,1152]{1,0:T(8,128)(2,1)S(1)}, u32[]{:S(2)}, u32[]{:S(2)}) collective-permute-start(bf16[256,1152]{1,0:T(8,128)(2,1)} %get-tuple-element.43), channel_id=1, source_target_pairs={{0,3},{1,2},{2,1},{3,0},{4,7},{5,6},{6,5},{7,4},{8,11},{9,10},{10,... | collective-permute-start | bytes 1769480 | tf_op jit(solution)/shard_map/ppermute | solution.py:433
  17.3 36.1 %collective-permute-start.10 = (bf16[128,1024]{1,0:T(8,128)(2,1)S(1)}, bf16[128,1024]{1,0:T(8,128)(2,1)S(1)}, u32[]{:S(2)}, u32[]{:S(2)}) collective-permute-start(bf16[128,1024]{1,0:T(8,128)(2,1)S(1)} %get-tuple-element.68), channel_id=1, source_target_pairs={{0,4},{1,5},{2,6},{3,7},{4,0},{5,1},{6,2},{7,3},{8,12},{9,13},{10,... | collective-permute-start | bytes 786440 | tf_op jit(solution)/shard_map/ppermute | solution.py:433
  17.4 1.8 collective-permute-start.24
  20.0 3.1 %collective-permute-start.25 = (f32[8,1024]{1,0:T(8,128)S(1)}, f32[8,1024]{1,0:T(8,128)S(1)}, u32[]{:S(2)}, u32[]{:S(2)}) collective-permute-start(f32[8,1024]{1,0:T(8,128)S(1)} %add.113), channel_id=1, source_target_pairs={{0,8},{1,9},{2,10},{3,11},{4,12},{5,13},{6,14},{7,15},{8,0},{9,1},... | collective-permute-start | bytes 98312 | tf_op jit(solution)/shard_map/ppermute | solution.py:433
  23.0 3.1 %collective-permute-start.26 = (f32[8,1024]{1,0:T(8,128)S(1)}, f32[8,1024]{1,0:T(8,128)S(1)}, u32[]{:S(2)}, u32[]{:S(2)}) collective-permute-start(f32[8,1024]{1,0:T(8,128)S(1)} %add.114), channel_id=1, source_target_pairs={{0,16},{1,17},{2,18},{3,19},{4,20},{5,21},{6,22},{7,23},{8,24},{9,... | collective-permute-start | bytes 98312 | tf_op jit(solution)/shard_map/ppermute | solution.py:433
  26.1 23.4 %collective-permute-start.27 = (f32[8,1024]{1,0:T(8,128)S(1)}, f32[8,1024]{1,0:T(8,128)S(1)}, u32[]{:S(2)}, u32[]{:S(2)}) collective-permute-start(f32[8,1024]{1,0:T(8,128)S(1)} %add.115), channel_id=1, source_target_pairs={{0,2},{1,3},{2,0},{3,1},{4,6},{5,7},{6,4},{7,5},{8,10},{9,11},{10,... | collective-permute-start | bytes 98312 | tf_op jit(solution)/shard_map/ppermute | solution.py:433
  49.5 3.8 %collective-permute-start.28 = (f32[8,1024]{1,0:T(8,128)S(1)}, f32[8,1024]{1,0:T(8,128)S(1)}, u32[]{:S(2)}, u32[]{:S(2)}) collective-permute-start(f32[8,1024]{1,0:T(8,128)S(1)} %add.116), channel_id=1, source_target_pairs={{0,4},{1,5},{2,6},{3,7},{4,0},{5,1},{6,2},{7,3},{8,12},{9,13},{10,... | collective-permute-start | bytes 98312 | tf_op jit(solution)/shard_map/ppermute | solution.py:433
  53.3 10.8 %collective-permute-start.6 = (bf16[128,1024]{1,0:T(8,128)(2,1)S(1)}, bf16[128,1024]{1,0:T(8,128)(2,1)S(1)}, u32[]{:S(2)}, u32[]{:S(2)}) collective-permute-start(bf16[128,1024]{1,0:T(8,128)(2,1)S(1)} %get-tuple-element.69), channel_id=1, source_target_pairs={{0,4},{1,5},{2,6},{3,7},{4,0},{5,1},{6,2},{7,3},{8,12},{9,13},{10,... | collective-permute-start | bytes 786440 | tf_op jit(solution)/shard_map/ppermute | solution.py:433
  53.3 11.8 %collective-permute-start.12 = (bf16[128,1024]{1,0:T(8,128)(2,1)S(1)}, bf16[128,1024]{1,0:T(8,128)(2,1)S(1)}, u32[]{:S(2)}, u32[]{:S(2)}) collective-permute-start(bf16[128,1024]{1,0:T(8,128)(2,1)S(1)} %collective-permute-done.10.refs_7_), channel_id=1, source_target_pairs={{0,16},{1,17},{2,18},{3,19},{4,20},{5,21},{6,22},{7,23},{8,24},{9,... | collective-permute-start | bytes 786440 | tf_op jit(solution)/shard_map/ppermute | solution.py:433
  64.1 13.1 %collective-permute-start.11 = (bf16[128,1024]{1,0:T(8,128)(2,1)S(1)}, bf16[128,1024]{1,0:T(8,128)(2,1)S(1)}, u32[]{:S(2)}, u32[]{:S(2)}) collective-permute-start(bf16[128,1024]{1,0:T(8,128)(2,1)S(1)} %collective-permute-done.10.refs_7_), channel_id=1, source_target_pairs={{0,8},{1,9},{2,10},{3,11},{4,12},{5,13},{6,14},{7,15},{8,0},{9,1},... | collective-permute-start | bytes 786440 | tf_op jit(solution)/shard_map/ppermute | solution.py:433
  65.1 11.0 %collective-permute-start.7 = (bf16[128,1024]{1,0:T(8,128)(2,1)S(1)}, bf16[128,1024]{1,0:T(8,128)(2,1)S(1)}, u32[]{:S(2)}, u32[]{:S(2)}) collective-permute-start(bf16[128,1024]{1,0:T(8,128)(2,1)S(1)} %collective-permute-done.6.refs_3_), channel_id=1, source_target_pairs={{0,8},{1,9},{2,10},{3,11},{4,12},{5,13},{6,14},{7,15},{8,0},{9,1},... | collective-permute-start | bytes 786440 | tf_op jit(solution)/shard_map/ppermute | solution.py:433
  65.5 12.9 %collective-permute-start.15 = (bf16[128,1024]{1,0:T(8,128)(2,1)S(1)}, bf16[128,1024]{1,0:T(8,128)(2,1)S(1)}, u32[]{:S(2)}, u32[]{:S(2)}) collective-permute-start(bf16[128,1024]{1,0:T(8,128)(2,1)S(1)} %collective-permute-done.6.refs_3_), channel_id=1, source_target_pairs={{0,2},{1,3},{2,0},{3,1},{4,6},{5,7},{6,4},{7,5},{8,10},{9,11},{10,... | collective-permute-start | bytes 786440 | tf_op jit(solution)/shard_map/ppermute | solution.py:433
  70.7 11.2 %collective-permute-start.19 = (bf16[128,1024]{1,0:T(8,128)(2,1)S(1)}, bf16[128,1024]{1,0:T(8,128)(2,1)S(1)}, u32[]{:S(2)}, u32[]{:S(2)}) collective-permute-start(bf16[128,1024]{1,0:T(8,128)(2,1)S(1)} %collective-permute-done.10.refs_7_), channel_id=1, source_target_pairs={{0,2},{1,3},{2,0},{3,1},{4,6},{5,7},{6,4},{7,5},{8,10},{9,11},{10,... | collective-permute-start | bytes 786440 | tf_op jit(solution)/shard_map/ppermute | solution.py:433
  71.4 13.0 %copy-start.2 = (bf16[3,256,1152]{2,1,0:T(8,128)(2,1)S(1)}, bf16[3,256,1152]{2,1,0:T(8,128)(2,1)}, u32[]{:S(2)}) copy-start(bf16[3,256,1152]{2,1,0:T(8,128)(2,1)} %get-tuple-element.40.refs_1_) | copy-start | bytes 5308420
  76.2 16.8 %collective-permute-start.8 = (bf16[128,1024]{1,0:T(8,128)(2,1)S(1)}, bf16[128,1024]{1,0:T(8,128)(2,1)S(1)}, u32[]{:S(2)}, u32[]{:S(2)}) collective-permute-start(bf16[128,1024]{1,0:T(8,128)(2,1)S(1)} %collective-permute-done.6.refs_3_), channel_id=1, source_target_pairs={{0,16},{1,17},{2,18},{3,19},{4,20},{5,21},{6,22},{7,23},{8,24},{9,... | collective-permute-start | bytes 786440 | tf_op jit(solution)/shard_map/ppermute | solution.py:433
  77.2 16.1 %collective-permute-start.13 = (bf16[128,1024]{1,0:T(8,128)(2,1)S(1)}, bf16[128,1024]{1,0:T(8,128)(2,1)S(1)}, u32[]{:S(2)}, u32[]{:S(2)}) collective-permute-start(bf16[128,1024]{1,0:T(8,128)(2,1)S(1)} %collective-permute-done.12.refs_9_), channel_id=1, source_target_pairs={{0,8},{1,9},{2,10},{3,11},{4,12},{5,13},{6,14},{7,15},{8,0},{9,1},... | collective-permute-start | bytes 786440 | tf_op jit(solution)/shard_map/ppermute | solution.py:433
  78.4 17.6 %collective-permute-start.9 = (bf16[128,1024]{1,0:T(8,128)(2,1)S(1)}, bf16[128,1024]{1,0:T(8,128)(2,1)S(1)}, u32[]{:S(2)}, u32[]{:S(2)}) collective-permute-start(bf16[128,1024]{1,0:T(8,128)(2,1)S(1)} %collective-permute-done.7.refs_4_), channel_id=1, source_target_pairs={{0,16},{1,17},{2,18},{3,19},{4,20},{5,21},{6,22},{7,23},{8,24},{9,... | collective-permute-start | bytes 786440 | tf_op jit(solution)/shard_map/ppermute | solution.py:433
  81.9 11.6 %collective-permute-start.16 = (bf16[128,1024]{1,0:T(8,128)(2,1)S(1)}, bf16[128,1024]{1,0:T(8,128)(2,1)S(1)}, u32[]{:S(2)}, u32[]{:S(2)}) collective-permute-start(bf16[128,1024]{1,0:T(8,128)(2,1)S(1)} %collective-permute-done.15.refs_3_), channel_id=1, source_target_pairs={{0,8},{1,9},{2,10},{3,11},{4,12},{5,13},{6,14},{7,15},{8,0},{9,1},... | collective-permute-start | bytes 786440 | tf_op jit(solution)/shard_map/ppermute | solution.py:433
  83.1 11.7 %collective-permute-start.21 = (bf16[128,1024]{1,0:T(8,128)(2,1)S(1)}, bf16[128,1024]{1,0:T(8,128)(2,1)S(1)}, u32[]{:S(2)}, u32[]{:S(2)}) collective-permute-start(bf16[128,1024]{1,0:T(8,128)(2,1)S(1)} %collective-permute-done.19.refs_7_), channel_id=1, source_target_pairs={{0,16},{1,17},{2,18},{3,19},{4,20},{5,21},{6,22},{7,23},{8,24},{9,... | collective-permute-start | bytes 786440 | tf_op jit(solution)/shard_map/ppermute | solution.py:433
  93.0 10.9 %collective-permute-start.17 = (bf16[128,1024]{1,0:T(8,128)(2,1)S(1)}, bf16[128,1024]{1,0:T(8,128)(2,1)S(1)}, u32[]{:S(2)}, u32[]{:S(2)}) collective-permute-start(bf16[128,1024]{1,0:T(8,128)(2,1)S(1)} %collective-permute-done.15.refs_3_), channel_id=1, source_target_pairs={{0,16},{1,17},{2,18},{3,19},{4,20},{5,21},{6,22},{7,23},{8,24},{9,... | collective-permute-start | bytes 786440 | tf_op jit(solution)/shard_map/ppermute | solution.py:433
  93.3 15.7 %collective-permute-start.20 = (bf16[128,1024]{1,0:T(8,128)(2,1)S(1)}, bf16[128,1024]{1,0:T(8,128)(2,1)S(1)}, u32[]{:S(2)}, u32[]{:S(2)}) collective-permute-start(bf16[128,1024]{1,0:T(8,128)(2,1)S(1)} %collective-permute-done.19.refs_7_), channel_id=1, source_target_pairs={{0,8},{1,9},{2,10},{3,11},{4,12},{5,13},{6,14},{7,15},{8,0},{9,1},... | collective-permute-start | bytes 786440 | tf_op jit(solution)/shard_map/ppermute | solution.py:433
  93.6 20.0 %collective-permute-start.18 = (bf16[128,1024]{1,0:T(8,128)(2,1)S(1)}, bf16[128,1024]{1,0:T(8,128)(2,1)S(1)}, u32[]{:S(2)}, u32[]{:S(2)}) collective-permute-start(bf16[128,1024]{1,0:T(8,128)(2,1)S(1)} %collective-permute-done.16.refs_4_), channel_id=1, source_target_pairs={{0,16},{1,17},{2,18},{3,19},{4,20},{5,21},{6,22},{7,23},{8,24},{9,... | collective-permute-start | bytes 786440 | tf_op jit(solution)/shard_map/ppermute | solution.py:433
  94.8 20.0 %collective-permute-start.22 = (bf16[128,1024]{1,0:T(8,128)(2,1)S(1)}, bf16[128,1024]{1,0:T(8,128)(2,1)S(1)}, u32[]{:S(2)}, u32[]{:S(2)}) collective-permute-start(bf16[128,1024]{1,0:T(8,128)(2,1)S(1)} %collective-permute-done.21.refs_9_), channel_id=1, source_target_pairs={{0,8},{1,9},{2,10},{3,11},{4,12},{5,13},{6,14},{7,15},{8,0},{9,1},... | collective-permute-start | bytes 786440 | tf_op jit(solution)/shard_map/ppermute | solution.py:433
  96.0 27.4 %collective-permute-start.29 = (bf16[2,256,512]{2,1,0:T(8,128)(2,1)S(1)}, bf16[2,256,512]{2,1,0:T(8,128)(2,1)S(1)}, u32[]{:S(2)}, u32[]{:S(2)}) collective-permute-start(bf16[2,256,512]{2,1,0:T(8,128)(2,1)S(1)} %get-tuple-element.57), channel_id=1, source_target_pairs={{0,8},{1,9},{2,10},{3,11},{4,12},{5,13},{6,14},{7,15},{8,0},{9,1},... | collective-permute-start | bytes 1572872 | tf_op jit(solution)/shard_map/ppermute | solution.py:433
  103.9 61.3 %collective-permute-start.4 = (bf16[256,1152]{1,0:T(8,128)(2,1)S(1)}, bf16[256,1152]{1,0:T(8,128)(2,1)S(1)}, u32[]{:S(2)}, u32[]{:S(2)}) collective-permute-start(bf16[256,1152]{1,0:T(8,128)(2,1)S(1)} %get-tuple-element.47), channel_id=1, source_target_pairs={{0,2},{1,3},{2,0},{3,1},{4,6},{5,7},{6,4},{7,5},{8,10},{9,11},{10,... | collective-permute-start | bytes 1769480 | tf_op jit(solution)/shard_map/ppermute | solution.py:433
  109.0 56.8 %collective-permute-start.5 = (bf16[256,1152]{1,0:T(8,128)(2,1)S(1)}, bf16[256,1152]{1,0:T(8,128)(2,1)S(1)}, u32[]{:S(2)}, u32[]{:S(2)}) collective-permute-start(bf16[256,1152]{1,0:T(8,128)(2,1)S(1)} %get-tuple-element.48), channel_id=1, source_target_pairs={{0,3},{1,2},{2,1},{3,0},{4,7},{5,6},{6,5},{7,4},{8,11},{9,10},{10,... | collective-permute-start | bytes 1769480 | tf_op jit(solution)/shard_map/ppermute | solution.py:433
  113.6 13.1 %collective-permute-start.31 = (bf16[2,256,512]{2,1,0:T(8,128)(2,1)S(1)}, bf16[2,256,512]{2,1,0:T(8,128)(2,1)S(1)}, u32[]{:S(2)}, u32[]{:S(2)}) collective-permute-start(bf16[2,256,512]{2,1,0:T(8,128)(2,1)S(1)} %get-tuple-element.59), channel_id=1, source_target_pairs={{0,16},{1,17},{2,18},{3,19},{4,20},{5,21},{6,22},{7,23},{8,24},{9,... | collective-permute-start | bytes 1572872 | tf_op jit(solution)/shard_map/ppermute | solution.py:433
  114.8 13.9 %collective-permute-start.33 = (bf16[2,256,512]{2,1,0:T(8,128)(2,1)S(1)}, bf16[2,256,512]{2,1,0:T(8,128)(2,1)S(1)}, u32[]{:S(2)}, u32[]{:S(2)}) collective-permute-start(bf16[2,256,512]{2,1,0:T(8,128)(2,1)S(1)} %get-tuple-element.61), channel_id=1, source_target_pairs={{0,8},{1,9},{2,10},{3,11},{4,12},{5,13},{6,14},{7,15},{8,0},{9,1},... | collective-permute-start | bytes 1572872 | tf_op jit(solution)/shard_map/ppermute | solution.py:433
  123.4 14.6 %collective-permute-start.35 = (bf16[2,256,512]{2,1,0:T(8,128)(2,1)S(1)}, bf16[2,256,512]{2,1,0:T(8,128)(2,1)S(1)}, u32[]{:S(2)}, u32[]{:S(2)}) collective-permute-start(bf16[2,256,512]{2,1,0:T(8,128)(2,1)S(1)} %get-tuple-element.63), channel_id=1, source_target_pairs={{0,16},{1,17},{2,18},{3,19},{4,20},{5,21},{6,22},{7,23},{8,24},{9,... | collective-permute-start | bytes 1572872 | tf_op jit(solution)/shard_map/ppermute | solution.py:433
  126.7 13.4 %collective-permute-start.38 = (bf16[2,256,512]{2,1,0:T(8,128)(2,1)S(1)}, bf16[2,256,512]{2,1,0:T(8,128)(2,1)S(1)}, u32[]{:S(2)}, u32[]{:S(2)}) collective-permute-start(bf16[2,256,512]{2,1,0:T(8,128)(2,1)S(1)} %get-tuple-element.65), channel_id=1, source_target_pairs={{0,8},{1,9},{2,10},{3,11},{4,12},{5,13},{6,14},{7,15},{8,0},{9,1},... | collective-permute-start | bytes 1572872 | tf_op jit(solution)/shard_map/ppermute | solution.py:433
  128.7 20.4 %collective-permute-start.40 = (bf16[2,256,512]{2,1,0:T(8,128)(2,1)S(1)}, bf16[2,256,512]{2,1,0:T(8,128)(2,1)S(1)}, u32[]{:S(2)}, u32[]{:S(2)}) collective-permute-start(bf16[2,256,512]{2,1,0:T(8,128)(2,1)S(1)} %get-tuple-element.67), channel_id=1, source_target_pairs={{0,16},{1,17},{2,18},{3,19},{4,20},{5,21},{6,22},{7,23},{8,24},{9,... | collective-permute-start | bytes 1572872 | tf_op jit(solution)/shard_map/ppermute | solution.py:433
  137.9 29.1 %collective-permute-start.23 = (bf16[256,1152]{1,0:T(8,128)(2,1)S(1)}, bf16[256,1152]{1,0:T(8,128)(2,1)S(1)}, u32[]{:S(2)}, u32[]{:S(2)}) collective-permute-start(bf16[256,1152]{1,0:T(8,128)(2,1)S(1)} %get-tuple-element.52), channel_id=1, source_target_pairs={{0,1},{1,0},{2,3},{3,2},{4,5},{5,4},{6,7},{7,6},{8,9},{9,8},{10,11... | collective-permute-start | bytes 1769480 | tf_op jit(solution)/shard_map/ppermute | solution.py:433
  140.1 14.7 %collective-permute-start.34 = (bf16[256,512]{1,0:T(8,128)(2,1)S(1)}, bf16[256,512]{1,0:T(8,128)(2,1)S(1)}, u32[]{:S(2)}, u32[]{:S(2)}) collective-permute-start(bf16[256,512]{1,0:T(8,128)(2,1)S(1)} %fusion.9), channel_id=1, source_target_pairs={{0,16},{1,17},{2,18},{3,19},{4,20},{5,21},{6,22},{7,23},{8,24},{9,... | collective-permute-start | bytes 786440 | tf_op jit(solution)/shard_map/ppermute | solution.py:433
  149.2 7.0 %collective-permute-start.36 = (bf16[256,512]{1,0:T(8,128)(2,1)S(1)}, bf16[256,512]{1,0:T(8,128)(2,1)S(1)}, u32[]{:S(2)}, u32[]{:S(2)}) collective-permute-start(bf16[256,512]{1,0:T(8,128)(2,1)S(1)} %fusion.10), channel_id=1, source_target_pairs={{0,8},{1,9},{2,10},{3,11},{4,12},{5,13},{6,14},{7,15},{8,0},{9,1},... | collective-permute-start | bytes 786440 | tf_op jit(solution)/shard_map/ppermute | solution.py:433
  154.8 6.6 %collective-permute-start.39 = (bf16[256,512]{1,0:T(8,128)(2,1)S(1)}, bf16[256,512]{1,0:T(8,128)(2,1)S(1)}, u32[]{:S(2)}, u32[]{:S(2)}) collective-permute-start(bf16[256,512]{1,0:T(8,128)(2,1)S(1)} %fusion.11), channel_id=1, source_target_pairs={{0,16},{1,17},{2,18},{3,19},{4,20},{5,21},{6,22},{7,23},{8,24},{9,... | collective-permute-start | bytes 786440 | tf_op jit(solution)/shard_map/ppermute | solution.py:433
  156.1 7.4 %collective-permute-start.41 = (bf16[256,512]{1,0:T(8,128)(2,1)S(1)}, bf16[256,512]{1,0:T(8,128)(2,1)S(1)}, u32[]{:S(2)}, u32[]{:S(2)}) collective-permute-start(bf16[256,512]{1,0:T(8,128)(2,1)S(1)} %fusion.12), channel_id=1, source_target_pairs={{0,8},{1,9},{2,10},{3,11},{4,12},{5,13},{6,14},{7,15},{8,0},{9,1},... | collective-permute-start | bytes 786440 | tf_op jit(solution)/shard_map/ppermute | solution.py:433
  157.5 14.1 %copy-start.1 = (bf16[1024,8]{0,1:T(8,128)(2,1)S(1)}, bf16[1024,8]{0,1:T(8,128)(2,1)}, u32[]{:S(2)}) copy-start(bf16[1024,8]{0,1:T(8,128)(2,1)} %param.10) | copy-start | bytes 49156
  157.5 14.1 %copy-start.3 = (s32[1,1024]{1,0:T(1,128)S(1)}, s32[1,1024]{1,0:T(1,128)}, u32[]{:S(2)}) copy-start(s32[1,1024]{1,0:T(1,128)} %get-tuple-element.36.key_ref.refs_0_) | copy-start | bytes 12292
  157.5 14.1 %copy-start.4 = (bf16[8,1024]{1,0:T(8,128)(2,1)S(1)}, bf16[8,1024]{1,0:T(8,128)(2,1)}, u32[]{:S(2)}) copy-start(bf16[8,1024]{1,0:T(8,128)(2,1)} %get-tuple-element.39.refs_2_) | copy-start | bytes 49156
  157.5 14.1 %copy-start.5 = (f32[1,1024]{1,0:T(1,128)S(1)}, f32[1,1024]{1,0:T(1,128)}, u32[]{:S(2)}) copy-start(f32[1,1024]{1,0:T(1,128)} %get-tuple-element.38.refs_1_) | copy-start | bytes 12292
  161.4 5.6 %collective-permute-start.14 = (bf16[256,1152]{1,0:T(8,128)(2,1)S(1)}, bf16[256,1152]{1,0:T(8,128)(2,1)S(1)}, u32[]{:S(2)}, u32[]{:S(2)}) collective-permute-start(bf16[256,1152]{1,0:T(8,128)(2,1)S(1)} %get-tuple-element.50), channel_id=1, source_target_pairs={{0,1},{1,0},{2,3},{3,2},{4,5},{5,4},{6,7},{7,6},{8,9},{9,8},{10,11... | collective-permute-start | bytes 1769480 | tf_op jit(solution)/shard_map/ppermute | solution.py:433
  163.5 8.1 %collective-permute-start.3 = (bf16[256,1152]{1,0:T(8,128)(2,1)S(1)}, bf16[256,1152]{1,0:T(8,128)(2,1)S(1)}, u32[]{:S(2)}, u32[]{:S(2)}) collective-permute-start(bf16[256,1152]{1,0:T(8,128)(2,1)S(1)} %get-tuple-element.46), channel_id=1, source_target_pairs={{0,1},{1,0},{2,3},{3,2},{4,5},{5,4},{6,7},{7,6},{8,9},{9,8},{10,11... | collective-permute-start | bytes 1769480 | tf_op jit(solution)/shard_map/ppermute | solution.py:433
  165.2 15.9 %collective-permute-start.30 = (bf16[256,512]{1,0:T(8,128)(2,1)S(1)}, bf16[256,512]{1,0:T(8,128)(2,1)S(1)}, u32[]{:S(2)}, u32[]{:S(2)}) collective-permute-start(bf16[256,512]{1,0:T(8,128)(2,1)S(1)} %fusion.7), channel_id=1, source_target_pairs={{0,16},{1,17},{2,18},{3,19},{4,20},{5,21},{6,22},{7,23},{8,24},{9,... | collective-permute-start | bytes 786440 | tf_op jit(solution)/shard_map/ppermute | solution.py:433
  165.8 15.4 %collective-permute-start.32 = (bf16[256,512]{1,0:T(8,128)(2,1)S(1)}, bf16[256,512]{1,0:T(8,128)(2,1)S(1)}, u32[]{:S(2)}, u32[]{:S(2)}) collective-permute-start(bf16[256,512]{1,0:T(8,128)(2,1)S(1)} %fusion.8), channel_id=1, source_target_pairs={{0,8},{1,9},{2,10},{3,11},{4,12},{5,13},{6,14},{7,15},{8,0},{9,1},... | collective-permute-start | bytes 786440 | tf_op jit(solution)/shard_map/ppermute | solution.py:433
  167.0 33.4 %collective-permute-start.37 = (bf16[256,1024]{1,0:T(8,128)(2,1)S(1)}, bf16[256,1024]{1,0:T(8,128)(2,1)S(1)}, u32[]{:S(2)}, u32[]{:S(2)}) collective-permute-start(bf16[256,1024]{1,0:T(8,128)(2,1)S(1)} %pad_maximum_fusion), channel_id=1, source_target_pairs={{0,4},{1,5},{2,6},{3,7},{4,0},{5,1},{6,2},{7,3},{8,12},{9,13},{10,... | collective-permute-start | bytes 1572872 | tf_op jit(solution)/shard_map/ppermute | solution.py:433
  167.1 48.4 %collective-permute-start.42 = (bf16[256,1024]{1,0:T(8,128)(2,1)S(1)}, bf16[256,1024]{1,0:T(8,128)(2,1)S(1)}, u32[]{:S(2)}, u32[]{:S(2)}) collective-permute-start(bf16[256,1024]{1,0:T(8,128)(2,1)S(1)} %pad_maximum_fusion.1), channel_id=1, source_target_pairs={{0,6},{1,7},{2,4},{3,5},{4,2},{5,3},{6,0},{7,1},{8,14},{9,15},{10,... | collective-permute-start | bytes 1572872 | tf_op jit(solution)/shard_map/ppermute | solution.py:433
  (1 other events, 11.0 us)
